TPU v7x, 512 devices: a whole 4x4x16 slice. The times are simulated.
512 devices in a mesh: seq: 128 (over z, y, core), head: 4 (over x).
Axes of the slice: x: 4, y: 4, z: 16, core: 2. Of those that a mesh axis runs over, the one named last changes fastest.
Arguments:
- queries: bfloat16 [16384, 1024], P('seq', 'head'), may hold values from -8 to 8
- keys: bfloat16 [16384, 1024], P('seq', 'head'), may hold values from -8 to 8
- values: bfloat16 [16384, 1024], P('seq', 'head'), may hold values from -6 to 6
- out_grad: bfloat16 [16384, 1024], P('seq', 'head'), may hold values from -6 to 6
- rel_emb: bfloat16 [512, 1024], replicated, may hold values from -6 to 6
- w_query: bfloat16 [1024, 1024], P(None, 'head'), may hold values from -0.1875 to 0.1875
- w_key: bfloat16 [1024, 1024], P(None, 'head'), may hold values from -0.1875 to 0.1875
- doc_lengths: int32 [64], replicated, may hold values from 1 to 512, 16384 in all
- bucket_table: int32 [1024], replicated, may hold values from 0 to 511, as said below
Outputs:
- query_grad: bfloat16 [16384, 1024], P('seq', 'head')
- key_grad: bfloat16 [16384, 1024], P('seq', 'head')
- value_grad: bfloat16 [16384, 1024], P('seq', 'head')
- rel_emb_grad: float32 [512, 1024], P(None, 'head')
- w_query_grad: float32 [1024, 1024], P('seq', 'head')
- w_key_grad: float32 [1024, 1024], P('seq', 'head')
Inputs may be any that keep to these rules, and one draw needn't show every extreme that they name: `doc_lengths`: the lengths sum to 16384 and the longest is exactly 512. `bucket_table`: entry o is the bucket of the relative offset o - 512; entries never fall as o grows, and equal o - 512 + 512 // 2 wherever o - 512 lies between -128 and 128.
All inputs are finite; a program needn't handle non-finite values.
Results may differ from a plain program's by a relative error of at most 0.01.
Values may be sent and summed in bfloat16 or wider, within the bound.
A program may use at most 64 MiB of HBM per device.

v0:
```python
import math

import jax
import jax.numpy as jnp
from jax import lax
from jax.sharding import Mesh
from jax.sharding import PartitionSpec as P

HD = 64
SPAN = 4
SEQ = ("seq_0", "seq_1", "seq_2")


masked_score = -1e30


def shifted(block, axis, distance):
    devices = range(lax.axis_size(axis))
    route = [(i - distance, i) for i in devices if i - distance in devices]
    return lax.ppermute(block, axis, route)


def split_up(shard, dim, count):
    before, after = (shard.shape[:dim], shard.shape[dim + 1 :])
    return jnp.moveaxis(shard.reshape(*before, count, -1, *after), dim, 0)


def summed_on_arrival(shard, axis, dim):
    tiles = split_up(shard, dim, lax.axis_size(axis))
    arrived = lax.all_to_all(tiles, axis, split_axis=0, concat_axis=0, tiled=True)
    return arrived.sum(axis=0)


def sum_in_two_steps(shard, axes, dim):
    far, near = axes
    tiles = split_up(shard, dim, lax.axis_size(far))
    nearer = summed_on_arrival(tiles, near, dim + 1)
    arrived = lax.all_to_all(nearer, far, split_axis=0, concat_axis=0, tiled=True)
    return arrived.sum(axis=0)


def padded_to(lines, count):
    spare = -lines.shape[0] % count
    if not spare:
        return lines
    return jnp.concatenate([lines, jnp.zeros((spare, *lines.shape[1:]), lines.dtype)])


def sent_to_all(shard, axis):
    copies = jnp.broadcast_to(shard, (lax.axis_size(axis), *shard.shape))
    return lax.all_to_all(copies, axis, split_axis=0, concat_axis=0, tiled=True)


def in_order(tiles, dim):
    lengths = list(tiles.shape[1:])
    lengths[dim] *= tiles.shape[0]
    return jnp.moveaxis(tiles, 0, dim).reshape(lengths)


def whole_of(shard, axes, dim):
    far, near = axes
    tiles = sent_to_all(sent_to_all(shard, far), near)
    return in_order(tiles.swapaxes(0, 1).reshape(-1, *shard.shape), dim)


def sum_by_parts(shard, axes):
    lines = shard.reshape(-1)
    own = sum_in_two_steps(
        padded_to(lines, lax.axis_size(axes[0]) * lax.axis_size(axes[1])), axes, 0
    )
    whole = whole_of(own, axes, 0)
    return whole[: len(lines)].reshape(shard.shape)


def sum_at_owner(shard, axis, dim):
    tiles = split_up(shard, dim, lax.axis_size(axis))
    arrived = lax.all_to_all(tiles, axis, split_axis=0, concat_axis=0, tiled=True)
    return arrived.astype(jnp.float32).sum(axis=0)


def contract(left, right, left_dim, right_dim):
    return lax.dot_general(
        left, right, (((left_dim,), (right_dim,)), ((), ())), preferred_element_type=jnp.float32
    )


def doc_index(position, doc_ends, extent):
    inside = (position >= 0) & (position < extent)
    owner = jnp.sum((doc_ends[None, :] <= position[:, None]).astype(jnp.int32), axis=1)
    return jnp.where(inside, owner, -1)


def same_document(row_pos, col_pos, doc_ends, extent):
    return (
        doc_index(row_pos, doc_ends, extent)[:, None]
        == doc_index(col_pos, doc_ends, extent)[None, :]
    )


def tile_tables(bucket_table, shift, rows, buckets):
    offset_span = bucket_table.shape[0] // 2
    spread = jnp.arange(2 * rows - 1, dtype=jnp.int32) - (rows - 1)
    ahead_index = bucket_table[jnp.clip(shift - spread + offset_span, 0, 2 * offset_span - 1)]
    behind_index = bucket_table[jnp.clip(offset_span - shift - spread, 0, 2 * offset_span - 1)]
    bucket_ids = jnp.arange(buckets, dtype=jnp.int32)[None, :]
    ahead_onehot = (ahead_index[:, None] == bucket_ids).astype(jnp.bfloat16)
    behind_onehot = (behind_index[:, None] == bucket_ids).astype(jnp.bfloat16)
    return (ahead_index, behind_index, ahead_onehot, behind_onehot)


def skew_in(spread, width):
    rows = spread.shape[0]
    line = rows + width - 1
    flat = jnp.pad(spread, ((0, 0), (0, 1))).reshape(-1)
    return flat[rows - 1 : rows - 1 + rows * line].reshape(rows, line)[:, :width]


def skew_out(dense):
    rows, width = dense.shape
    line = rows + width - 1
    padded = jnp.pad(dense, ((0, 0), (0, rows - 1))).reshape(-1)
    flat = jnp.pad(padded, (rows - 1, 1))
    return flat.reshape(rows, line + 1)[:, :line]


def tile_scores(
    query_rows, key_rows, pos_keys, pos_queries, ahead_onehot, behind_onehot, score_scale
):
    content = contract(query_rows, key_rows, 1, 1)
    ahead_band = contract(ahead_onehot, pos_keys, 1, 0).astype(jnp.bfloat16)
    behind_band = contract(behind_onehot, pos_queries, 1, 0).astype(jnp.bfloat16)
    query_term = skew_in(contract(query_rows, ahead_band, 1, 1), key_rows.shape[0])
    key_term = skew_in(contract(key_rows, behind_band, 1, 1), query_rows.shape[0]).T
    return score_scale * (content + query_term + key_term)


def query_side(
    query_rows,
    key_rows,
    value_rows,
    grad_rows,
    pos_keys,
    pos_queries,
    same_doc,
    tables,
    score_scale,
):
    tile_rows = query_rows.shape[0]
    tile_count = key_rows.shape[0] // tile_rows
    pieces = []
    for tile in range(tile_count):
        key_tile = key_rows[tile * tile_rows : (tile + 1) * tile_rows]
        pieces.append(
            tile_scores(
                query_rows,
                key_tile,
                pos_keys,
                pos_queries,
                tables[tile][2],
                tables[tile][3],
                score_scale,
            )
        )
    scores = jnp.where(same_doc, jnp.concatenate(pieces, 1), masked_score)
    row_max = jnp.max(scores, axis=1, keepdims=True)
    expd = jnp.where(same_doc, jnp.exp(scores - row_max), 0.0)
    row_sum = jnp.sum(expd, axis=1, keepdims=True)
    probs = expd / row_sum
    dprobs = contract(grad_rows, value_rows, 1, 1)
    row_dot = jnp.sum(probs * dprobs, axis=1, keepdims=True)
    dscores = probs * (dprobs - row_dot)
    dscores_low = dscores.astype(jnp.bfloat16)
    ahead_grad = jnp.zeros((tile_rows, pos_keys.shape[0]), jnp.float32)
    for tile in range(tile_count):
        band = dscores_low[:, tile * tile_rows : (tile + 1) * tile_rows]
        ahead_grad = ahead_grad + contract(skew_out(band), tables[tile][2], 1, 0)
    ahead_low = ahead_grad.astype(jnp.bfloat16)
    query_grad = score_scale * (
        contract(dscores_low, key_rows, 1, 0) + contract(ahead_low, pos_keys, 1, 0)
    )
    bucket_key = score_scale * contract(ahead_low, query_rows, 0, 0)
    probs_low = probs.astype(jnp.bfloat16)
    behind_parts = []
    for tile in range(tile_count):
        band = dscores_low[:, tile * tile_rows : (tile + 1) * tile_rows]
        behind_parts.append(contract(skew_out(band.T), tables[tile][3], 1, 0).astype(jnp.bfloat16))
    behind_low = jnp.concatenate(behind_parts, 0)
    key_grad = score_scale * (
        contract(dscores_low, query_rows, 0, 0) + contract(behind_low, pos_queries, 1, 0)
    )
    value_grad = contract(probs_low, grad_rows, 0, 0)
    bucket_query = score_scale * contract(behind_low, key_rows, 0, 0)
    return (query_grad, key_grad, value_grad, bucket_key, bucket_query)


def split_heads(matrix):
    return matrix.reshape(matrix.shape[0], matrix.shape[1] // HD, HD).transpose(1, 0, 2)


def join_heads(stacked):
    return stacked.transpose(1, 0, 2).reshape(stacked.shape[1], stacked.shape[0] * HD)


def body(queries, keys, values, out_grad, rel_emb, w_query, w_key, doc_lengths, bucket_table):
    tokens_dev = queries.shape[0]
    seq_count = lax.axis_size(SEQ)
    neighbours = min(SPAN, seq_count // 4)
    extent = tokens_dev * seq_count
    seq_index = lax.axis_index(SEQ)
    first_token = seq_index * tokens_dev
    score_scale = 1.0 / math.sqrt(3.0 * HD)
    pos_key = jnp.dot(rel_emb, w_key, preferred_element_type=jnp.float32).astype(jnp.bfloat16)
    pos_query = jnp.dot(rel_emb, w_query, preferred_element_type=jnp.float32).astype(jnp.bfloat16)
    doc_ends = jnp.cumsum(doc_lengths)
    buckets = rel_emb.shape[0]
    tables = [
        tile_tables(bucket_table, (neighbours - tile) * tokens_dev, tokens_dev, buckets)
        for tile in range(2 * neighbours + 1)
    ]
    hop_list = list(range(neighbours, 0, -1)) + list(range(-1, -neighbours - 1, -1))
    fetched = []
    for distance in hop_list:
        fetched.append(shifted((keys, values), SEQ, distance))
    lower_side = fetched[:neighbours]
    upper_side = fetched[neighbours:]
    key_window = jnp.concatenate(
        [pair[0] for pair in lower_side] + [keys] + [pair[0] for pair in upper_side], 0
    )
    value_window = jnp.concatenate(
        [pair[1] for pair in lower_side] + [values] + [pair[1] for pair in upper_side], 0
    )
    window = key_window.shape[0]
    query_pos = first_token + jnp.arange(tokens_dev, dtype=jnp.int32)
    window_pos = first_token - neighbours * tokens_dev + jnp.arange(window, dtype=jnp.int32)
    same_doc = same_document(query_pos, window_pos, doc_ends, extent)
    query_heads = split_heads(queries)
    grad_heads = split_heads(out_grad)
    pos_key_heads = split_heads(pos_key)
    pos_query_heads = split_heads(pos_query)

    def every_pair(operands):
        query_rows, key_rows, value_rows, grad_rows, pos_keys, pos_queries = operands
        return query_side(
            query_rows,
            key_rows,
            value_rows,
            grad_rows,
            pos_keys,
            pos_queries,
            same_doc,
            tables,
            score_scale,
        )

    query_grad, key_part, value_part, bucket_key, bucket_query = lax.map(
        every_pair,
        (
            query_heads,
            split_heads(key_window),
            split_heads(value_window),
            grad_heads,
            pos_key_heads,
            pos_query_heads,
        ),
    )
    key_flat = join_heads(key_part)
    value_flat = join_heads(value_part)
    key_total = key_flat[neighbours * tokens_dev : (neighbours + 1) * tokens_dev]
    value_total = value_flat[neighbours * tokens_dev : (neighbours + 1) * tokens_dev]
    for distance in hop_list:
        segment = neighbours - distance
        returned = (
            key_flat[segment * tokens_dev : (segment + 1) * tokens_dev],
            value_flat[segment * tokens_dev : (segment + 1) * tokens_dev],
        )
        arrived = shifted((returned[0], returned[1]), SEQ, -distance)
        key_total = key_total + arrived[0]
        value_total = value_total + arrived[1]
    key_grad = key_total.astype(jnp.bfloat16)
    value_grad = value_total.astype(jnp.bfloat16)
    query_out = join_heads(query_grad).astype(jnp.bfloat16)
    summed = (
        sum_by_parts(join_heads(bucket_key), (("seq_0", "seq_1"), "seq_2")),
        sum_by_parts(join_heads(bucket_query), (("seq_0", "seq_1"), "seq_2")),
    )
    bucket_key_low = summed[0].astype(jnp.bfloat16)
    bucket_query_low = summed[1].astype(jnp.bfloat16)
    rows_dev = rel_emb.shape[1] // seq_count
    rel_columns = lax.dynamic_slice_in_dim(rel_emb, seq_index * rows_dev, rows_dev, 1)
    w_key_grad = contract(rel_columns, bucket_key_low, 0, 0)
    w_query_grad = contract(rel_columns, bucket_query_low, 0, 0)
    rel_partial = contract(bucket_key_low, w_key, 1, 1) + contract(bucket_query_low, w_query, 1, 1)
    rel_emb_grad = sum_at_owner(rel_partial.astype(jnp.bfloat16), "head", 1)
    return (query_out, key_grad, value_grad, rel_emb_grad, w_query_grad, w_key_grad)


def solution(mesh):
    split = Mesh(
        mesh.devices.reshape(16, 4, 2, mesh.shape["head"]), ("seq_0", "seq_1", "seq_2", "head")
    )
    placed = (
        P(SEQ, "head"),
        P(SEQ, "head"),
        P(SEQ, "head"),
        P(SEQ, "head"),
        P(),
        P(None, "head"),
        P(None, "head"),
        P(),
        P(),
    )
    return jax.shard_map(
        body,
        mesh=split,
        in_specs=placed,
        out_specs=(
            P(SEQ, "head"),
            P(SEQ, "head"),
            P(SEQ, "head"),
            P(None, "head"),
            P(SEQ, "head"),
            P(SEQ, "head"),
        ),
        check_vma=False,
    )
```

profile of v0, /device:TPU:1, one launch (start us, length us, event | category | flops | bytes accessed | tf_op | source)
XLA Modules:
  0.0 541.6 jit_solution(16759092686333075120)
XLA Ops:
  1.7 6.3 %collective-permute-start.8 = (bf16[128,256]{0,1:T(8,128)(2,1)S(1)}, bf16[128,256]{0,1:T(8,128)(2,1)}, u32[]{:S(2)}, u32[]{:S(2)}) collective-permute-start(bf16[128,256]{0,1:T(8,128)(2,1)S(1)} %copy.181), channel_id=1, source_target_pairs={{0,16},{4,20},{8,24},{12,28},{16,32},{20,36},{24,40},{28,44},{32,4... | collective-permute-start | bytes 196616 | tf_op jit(solution)/shard_map/ppermute | solution.py:20
  46.4 7.0 %collective-permute-start = (bf16[128,256]{0,1:T(8,128)(2,1)S(1)}, bf16[128,256]{0,1:T(8,128)(2,1)S(1)}, u32[]{:S(2)}, u32[]{:S(2)}) collective-permute-start(bf16[128,256]{0,1:T(8,128)(2,1)S(1)} %copy.169), channel_id=1, source_target_pairs={{0,16},{4,20},{8,24},{12,28},{16,32},{20,36},{24,40},{28,44},{32,4... | collective-permute-start | bytes 196616 | tf_op jit(solution)/shard_map/ppermute | solution.py:20
  56.4 6.0 %collective-permute-start.1 = (bf16[128,256]{0,1:T(8,128)(2,1)S(1)}, bf16[128,256]{0,1:T(8,128)(2,1)S(1)}, u32[]{:S(2)}, u32[]{:S(2)}) collective-permute-start(bf16[128,256]{0,1:T(8,128)(2,1)S(1)} %copy.169), channel_id=1, source_target_pairs={{0,12},{4,16},{8,20},{12,24},{16,28},{20,32},{24,36},{28,40},{32,4... | collective-permute-start | bytes 196616 | tf_op jit(solution)/shard_map/ppermute | solution.py:20
  68.2 5.5 %collective-permute-start.3 = (bf16[128,256]{0,1:T(8,128)(2,1)S(1)}, bf16[128,256]{0,1:T(8,128)(2,1)S(1)}, u32[]{:S(2)}, u32[]{:S(2)}) collective-permute-start(bf16[128,256]{0,1:T(8,128)(2,1)S(1)} %copy.169), channel_id=1, source_target_pairs={{0,4},{4,8},{8,12},{12,16},{16,20},{20,24},{24,28},{28,32},{32,36}... | collective-permute-start | bytes 196616 | tf_op jit(solution)/shard_map/ppermute | solution.py:20
  83.9 4.7 collective-permute-done.6
  91.7 231.2 %while.22 = (s32[]{:T(128)}, bf16[4,128,64]{1,2,0:T(8,128)(2,1)}, f32[4,1152,64]{1,2,0:T(8,128)}, f32[4,1152,64]{1,2,0:T(8,128)}, f32[4,512,64]{1,2,0:T(8,128)},...) while((s32[]{:T(128)}, bf16[4,128,64]{1,2,0:T(8,128)(2,1)}, ...), condition=%wide.region_7.8_spmd.clone, body=%wide.region_3.7_spmd.clone.sunk | while | flops 1255631232 | bytes 64159832 | solution.py:255
  325.5 3.9 all_to_all.61
  331.8 4.2 all_to_all.62
  336.0 35.6 %all-to-all-start.1 = ((f32[64,1,1024]{2,1,0:T(1,128)}), f32[64,1,1024]{2,1,0:T(1,128)S(1)}, u32[]{:S(2)}, u32[]{:S(2)}) async-start(f32[64,1,1024]{2,1,0:T(1,128)} %all_to_all.40), calls=%async_computation.1 | async-start | bytes 524288 | tf_op jit(solution)/shard_map/all_to_all | solution.py:38
  372.6 19.2 %all-to-all-done.1 = f32[64,1,1024]{2,1,0:T(1,128)S(1)} async-done(((f32[64,1,1024]{2,1,0:T(1,128)}), f32[64,1,1024]{2,1,0:T(1,128)S(1)}, u32[]{:S(2)}, u32[]{:S(2)}) %all-to-all-start.1) | async-done | bytes 262176 | tf_op jit(solution)/shard_map/all_to_all | solution.py:38
  391.8 6.5 %all-to-all-start.5 = ((f32[64,1,1024]{2,1,0:T(1,128)}), f32[64,1,1024]{2,1,0:T(1,128)S(1)}, u32[]{:S(2)}, u32[]{:S(2)}) async-start(f32[64,1,1024]{2,1,0:T(1,128)} %all_to_all.46), calls=%async_computation.5 | async-start | bytes 524288 | tf_op jit(solution)/shard_map/all_to_all | solution.py:38
  401.3 16.0 %all-to-all-done.5 = f32[64,1,1024]{2,1,0:T(1,128)S(1)} async-done(((f32[64,1,1024]{2,1,0:T(1,128)}), f32[64,1,1024]{2,1,0:T(1,128)S(1)}, u32[]{:S(2)}, u32[]{:S(2)}) %all-to-all-start.5) | async-done | bytes 262176 | tf_op jit(solution)/shard_map/all_to_all | solution.py:38
  417.3 7.6 %all-to-all-start.2 = ((bf16[64,2,512]{2,1,0:T(2,128)(2,1)}), bf16[64,2,512]{2,1,0:T(2,128)(2,1)S(1)}, u32[]{:S(2)}, u32[]{:S(2)}) async-start(bf16[64,2,512]{2,1,0:T(2,128)(2,1)} %reshape.1002), calls=%async_computation.2 | async-start | bytes 262144 | tf_op jit(solution)/shard_map/all_to_all | solution.py:51
  433.5 4.2 collective-permute-start.28
  441.1 6.2 %all_to_all.63 = bf16[2,64,1024]{2,1,0:T(8,128)(2,1)S(1)} all-to-all(bf16[2,64,1024]{2,1,0:T(8,128)(2,1)S(1)} %broadcast_in_dim.134), channel_id=1, replica_groups=mesh['seq_0'=16,'seq_1'=4,'seq_2'=2,'head'=4] {'seq_2'}, dimensions={0} | all-to-all | bytes 524288 | tf_op jit(solution)/shard_map/all_to_all | solution.py:51
  447.3 18.5 %all-to-all-start.6 = ((bf16[64,2,512]{2,1,0:T(2,128)(2,1)}), bf16[64,2,512]{2,1,0:T(2,128)(2,1)}, u32[]{:S(2)}, u32[]{:S(2)}) async-start(bf16[64,2,512]{2,1,0:T(2,128)(2,1)} %reshape.1004), calls=%async_computation.6 | async-start | bytes 262144 | tf_op jit(solution)/shard_map/all_to_all | solution.py:51
  472.9 7.9 %all-to-all-done.6 = bf16[64,2,512]{2,1,0:T(2,128)(2,1)} async-done(((bf16[64,2,512]{2,1,0:T(2,128)(2,1)}), bf16[64,2,512]{2,1,0:T(2,128)(2,1)}, u32[]{:S(2)}, u32[]{:S(2)}) %all-to-all-start.6) | async-done | bytes 131104 | tf_op jit(solution)/shard_map/all_to_all | solution.py:51
  484.0 7.0 %all_to_all.64 = bf16[2,64,1024]{2,1,0:T(8,128)(2,1)S(1)} all-to-all(bf16[2,64,1024]{2,1,0:T(8,128)(2,1)S(1)} %broadcast_in_dim.136), channel_id=1, replica_groups=mesh['seq_0'=16,'seq_1'=4,'seq_2'=2,'head'=4] {'seq_2'}, dimensions={0} | all-to-all | bytes 524288 | tf_op jit(solution)/shard_map/all_to_all | solution.py:51
  493.7 4.4 collective-permute-start.30
  508.2 4.2 all-to-all-start.8
  514.4 3.8 collective-permute-start.20
  518.2 5.1 collective-permute-start.21
  523.4 4.8 collective-permute-start.22
  528.2 6.3 %collective-permute-start.23 = (f32[128,256]{0,1:T(8,128)S(1)}, f32[128,256]{0,1:T(8,128)}, u32[]{:S(2)}, u32[]{:S(2)}) collective-permute-start(f32[128,256]{0,1:T(8,128)S(1)} %bitcast.713), channel_id=1, source_target_pairs={{0,16},{4,20},{8,24},{12,28},{16,32},{20,36},{24,40},{28,44},{32,4... | collective-permute-start | bytes 393224 | tf_op jit(solution)/shard_map/ppermute | solution.py:20
  (1280 shorter events, 321.9 us)
Async XLA Ops:
  1.7 39.7 %collective-permute-start.8 = (bf16[128,256]{0,1:T(8,128)(2,1)S(1)}, bf16[128,256]{0,1:T(8,128)(2,1)}, u32[]{:S(2)}, u32[]{:S(2)}) collective-permute-start(bf16[128,256]{0,1:T(8,128)(2,1)S(1)} %copy.181), channel_id=1, source_target_pairs={{0,16},{4,20},{8,24},{12,28},{16,32},{20,36},{24,40},{28,44},{32,4... | collective-permute-start | bytes 196616 | tf_op jit(solution)/shard_map/ppermute | solution.py:20
  8.0 35.8 %collective-permute-start.9 = (bf16[128,256]{0,1:T(8,128)(2,1)S(1)}, bf16[128,256]{0,1:T(8,128)(2,1)S(1)}, u32[]{:S(2)}, u32[]{:S(2)}) collective-permute-start(bf16[128,256]{0,1:T(8,128)(2,1)S(1)} %copy.181), channel_id=1, source_target_pairs={{0,12},{4,16},{8,20},{12,24},{16,28},{20,32},{24,36},{28,40},{32,4... | collective-permute-start | bytes 196616 | tf_op jit(solution)/shard_map/ppermute | solution.py:20
  11.5 33.5 %collective-permute-start.10 = (bf16[128,256]{0,1:T(8,128)(2,1)S(1)}, bf16[128,256]{0,1:T(8,128)(2,1)S(1)}, u32[]{:S(2)}, u32[]{:S(2)}) collective-permute-start(bf16[128,256]{0,1:T(8,128)(2,1)S(1)} %copy.181), channel_id=1, source_target_pairs={{0,8},{4,12},{8,16},{12,20},{16,24},{20,28},{24,32},{28,36},{32,40... | collective-permute-start | bytes 196616 | tf_op jit(solution)/shard_map/ppermute | solution.py:20
  14.7 31.7 %collective-permute-start.11 = (bf16[128,256]{0,1:T(8,128)(2,1)S(1)}, bf16[128,256]{0,1:T(8,128)(2,1)S(1)}, u32[]{:S(2)}, u32[]{:S(2)}) collective-permute-start(bf16[128,256]{0,1:T(8,128)(2,1)S(1)} %copy.181), channel_id=1, source_target_pairs={{0,4},{4,8},{8,12},{12,16},{16,20},{20,24},{24,28},{28,32},{32,36}... | collective-permute-start | bytes 196616 | tf_op jit(solution)/shard_map/ppermute | solution.py:20
  16.7 60.4 %collective-permute-start.12 = (bf16[128,256]{0,1:T(8,128)(2,1)S(1)}, bf16[128,256]{0,1:T(8,128)(2,1)}, u32[]{:S(2)}, u32[]{:S(2)}) collective-permute-start(bf16[128,256]{0,1:T(8,128)(2,1)S(1)} %copy.181), channel_id=1, source_target_pairs={{4,0},{8,4},{12,8},{16,12},{20,16},{24,20},{28,24},{32,28},{36,32}... | collective-permute-start | bytes 196616 | tf_op jit(solution)/shard_map/ppermute | solution.py:20
  41.4 37.8 %collective-permute-start.13 = (bf16[128,256]{0,1:T(8,128)(2,1)S(1)}, bf16[128,256]{0,1:T(8,128)(2,1)S(1)}, u32[]{:S(2)}, u32[]{:S(2)}) collective-permute-start(bf16[128,256]{0,1:T(8,128)(2,1)S(1)} %copy.181), channel_id=1, source_target_pairs={{8,0},{12,4},{16,8},{20,12},{24,16},{28,20},{32,24},{36,28},{40,32... | collective-permute-start | bytes 196616 | tf_op jit(solution)/shard_map/ppermute | solution.py:20
  43.7 36.8 %collective-permute-start.14 = (bf16[128,256]{0,1:T(8,128)(2,1)S(1)}, bf16[128,256]{0,1:T(8,128)(2,1)S(1)}, u32[]{:S(2)}, u32[]{:S(2)}) collective-permute-start(bf16[128,256]{0,1:T(8,128)(2,1)S(1)} %copy.181), channel_id=1, source_target_pairs={{12,0},{16,4},{20,8},{24,12},{28,16},{32,20},{36,24},{40,28},{44,3... | collective-permute-start | bytes 196616 | tf_op jit(solution)/shard_map/ppermute | solution.py:20
  45.1 36.8 %collective-permute-start.15 = (bf16[128,256]{0,1:T(8,128)(2,1)S(1)}, bf16[128,256]{0,1:T(8,128)(2,1)S(1)}, u32[]{:S(2)}, u32[]{:S(2)}) collective-permute-start(bf16[128,256]{0,1:T(8,128)(2,1)S(1)} %copy.181), channel_id=1, source_target_pairs={{16,0},{20,4},{24,8},{28,12},{32,16},{36,20},{40,24},{44,28},{48,3... | collective-permute-start | bytes 196616 | tf_op jit(solution)/shard_map/ppermute | solution.py:20
  336.0 55.8 %all-to-all-start.1 = ((f32[64,1,1024]{2,1,0:T(1,128)}), f32[64,1,1024]{2,1,0:T(1,128)S(1)}, u32[]{:S(2)}, u32[]{:S(2)}) async-start(f32[64,1,1024]{2,1,0:T(1,128)} %all_to_all.40), calls=%async_computation.1 | async-start | bytes 524288 | tf_op jit(solution)/shard_map/all_to_all | solution.py:38
  391.8 25.5 %all-to-all-start.5 = ((f32[64,1,1024]{2,1,0:T(1,128)}), f32[64,1,1024]{2,1,0:T(1,128)S(1)}, u32[]{:S(2)}, u32[]{:S(2)}) async-start(f32[64,1,1024]{2,1,0:T(1,128)} %all_to_all.46), calls=%async_computation.5 | async-start | bytes 524288 | tf_op jit(solution)/shard_map/all_to_all | solution.py:38
  417.3 23.7 %all-to-all-start.2 = ((bf16[64,2,512]{2,1,0:T(2,128)(2,1)}), bf16[64,2,512]{2,1,0:T(2,128)(2,1)S(1)}, u32[]{:S(2)}, u32[]{:S(2)}) async-start(bf16[64,2,512]{2,1,0:T(2,128)(2,1)} %reshape.1002), calls=%async_computation.2 | async-start | bytes 262144 | tf_op jit(solution)/shard_map/all_to_all | solution.py:51
  425.9 41.3 %collective-permute-start.24 = (f32[128,256]{0,1:T(8,128)S(1)}, f32[128,256]{0,1:T(8,128)S(1)}, u32[]{:S(2)}, u32[]{:S(2)}) collective-permute-start(f32[128,256]{0,1:T(8,128)S(1)} %bitcast.722), channel_id=1, source_target_pairs={{16,0},{20,4},{24,8},{28,12},{32,16},{36,20},{40,24},{44,28},{48,3... | collective-permute-start | bytes 393224 | tf_op jit(solution)/shard_map/ppermute | solution.py:20
  427.2 66.5 %collective-permute-start.25 = (f32[128,256]{0,1:T(8,128)}, f32[128,256]{0,1:T(8,128)}, u32[]{:S(2)}, u32[]{:S(2)}) collective-permute-start(f32[128,256]{0,1:T(8,128)} %bitcast.37), channel_id=1, source_target_pairs={{12,0},{16,4},{20,8},{24,12},{28,16},{32,20},{36,24},{40,28},{44,3... | collective-permute-start | bytes 393224 | tf_op jit(solution)/shard_map/ppermute | solution.py:20
  428.5 69.6 %collective-permute-start.26 = (f32[128,256]{0,1:T(8,128)}, f32[128,256]{0,1:T(8,128)}, u32[]{:S(2)}, u32[]{:S(2)}) collective-permute-start(f32[128,256]{0,1:T(8,128)} %bitcast.38), channel_id=1, source_target_pairs={{8,0},{12,4},{16,8},{20,12},{24,16},{28,20},{32,24},{36,28},{40,32... | collective-permute-start | bytes 393224 | tf_op jit(solution)/shard_map/ppermute | solution.py:20
  429.8 71.7 %collective-permute-start.27 = (f32[128,256]{0,1:T(8,128)}, f32[128,256]{0,1:T(8,128)}, u32[]{:S(2)}, u32[]{:S(2)}) collective-permute-start(f32[128,256]{0,1:T(8,128)} %bitcast.39), channel_id=1, source_target_pairs={{4,0},{8,4},{12,8},{16,12},{20,16},{24,20},{28,24},{32,28},{36,32}... | collective-permute-start | bytes 393224 | tf_op jit(solution)/shard_map/ppermute | solution.py:20
  433.5 69.3 %collective-permute-start.28 = (f32[128,256]{0,1:T(8,128)}, f32[128,256]{0,1:T(8,128)}, u32[]{:S(2)}, u32[]{:S(2)}) collective-permute-start(f32[128,256]{0,1:T(8,128)} %bitcast.40), channel_id=1, source_target_pairs={{0,4},{4,8},{8,12},{12,16},{16,20},{20,24},{24,28},{28,32},{32,36}... | collective-permute-start | bytes 393224 | tf_op jit(solution)/shard_map/ppermute | solution.py:20
  447.3 33.5 %all-to-all-start.6 = ((bf16[64,2,512]{2,1,0:T(2,128)(2,1)}), bf16[64,2,512]{2,1,0:T(2,128)(2,1)}, u32[]{:S(2)}, u32[]{:S(2)}) async-start(bf16[64,2,512]{2,1,0:T(2,128)(2,1)} %reshape.1004), calls=%async_computation.6 | async-start | bytes 262144 | tf_op jit(solution)/shard_map/all_to_all | solution.py:51
  467.9 36.3 %collective-permute-start.29 = (f32[128,256]{0,1:T(8,128)}, f32[128,256]{0,1:T(8,128)}, u32[]{:S(2)}, u32[]{:S(2)}) collective-permute-start(f32[128,256]{0,1:T(8,128)} %bitcast.41), channel_id=1, source_target_pairs={{0,8},{4,12},{8,16},{12,20},{16,24},{20,28},{24,32},{28,36},{32,40... | collective-permute-start | bytes 393224 | tf_op jit(solution)/shard_map/ppermute | solution.py:20
  493.7 18.6 %collective-permute-start.30 = (f32[128,256]{0,1:T(8,128)}, f32[128,256]{0,1:T(8,128)}, u32[]{:S(2)}, u32[]{:S(2)}) collective-permute-start(f32[128,256]{0,1:T(8,128)} %bitcast.715), channel_id=1, source_target_pairs={{0,12},{4,16},{8,20},{12,24},{16,28},{20,32},{24,36},{28,40},{32,4... | collective-permute-start | bytes 393224 | tf_op jit(solution)/shard_map/ppermute | solution.py:20
  502.8 20.5 %collective-permute-start.17 = (f32[128,256]{0,1:T(8,128)}, f32[128,256]{0,1:T(8,128)}, u32[]{:S(2)}, u32[]{:S(2)}) collective-permute-start(f32[128,256]{0,1:T(8,128)} %bitcast.720), channel_id=1, source_target_pairs={{12,0},{16,4},{20,8},{24,12},{28,16},{32,20},{36,24},{40,28},{44,3... | collective-permute-start | bytes 393224 | tf_op jit(solution)/shard_map/ppermute | solution.py:20
  504.1 24.1 %collective-permute-start.18 = (f32[128,256]{0,1:T(8,128)}, f32[128,256]{0,1:T(8,128)}, u32[]{:S(2)}, u32[]{:S(2)}) collective-permute-start(f32[128,256]{0,1:T(8,128)} %bitcast.719), channel_id=1, source_target_pairs={{8,0},{12,4},{16,8},{20,12},{24,16},{28,20},{32,24},{36,28},{40,32... | collective-permute-start | bytes 393224 | tf_op jit(solution)/shard_map/ppermute | solution.py:20
  508.2 32.3 %all-to-all-start.8 = ((bf16[4,512,256]{2,1,0:T(8,128)(2,1)}), bf16[4,512,256]{2,1,0:T(8,128)(2,1)S(1)}, u32[]{:S(2)}, u32[]{:S(2)}) async-start(bf16[4,512,256]{2,1,0:T(8,128)(2,1)} %bitcast.435), calls=%async_computation.8 | async-start | bytes 2097152 | tf_op jit(solution)/shard_map/all_to_all | solution.py:77
  512.3 24.3 %collective-permute-start.19 = (f32[128,256]{0,1:T(8,128)S(1)}, f32[128,256]{0,1:T(8,128)}, u32[]{:S(2)}, u32[]{:S(2)}) collective-permute-start(f32[128,256]{0,1:T(8,128)S(1)} %bitcast.718), channel_id=1, source_target_pairs={{4,0},{8,4},{12,8},{16,12},{20,16},{24,20},{28,24},{32,28},{36,32}... | collective-permute-start | bytes 393224 | tf_op jit(solution)/shard_map/ppermute | solution.py:20
  514.4 22.2 %collective-permute-start.20 = (f32[128,256]{0,1:T(8,128)S(1)}, f32[128,256]{0,1:T(8,128)}, u32[]{:S(2)}, u32[]{:S(2)}) collective-permute-start(f32[128,256]{0,1:T(8,128)S(1)} %bitcast.717), channel_id=1, source_target_pairs={{0,4},{4,8},{8,12},{12,16},{16,20},{20,24},{24,28},{28,32},{32,36}... | collective-permute-start | bytes 393224 | tf_op jit(solution)/shard_map/ppermute | solution.py:20
  (95 other events, 721.5 us)
where the time goes:
time: 550 us; the launch traced here: 542 us
  starting transfers between devices  170 us (31%)
  local copies, waits for them, and re-layouts  132 us (24%)
  matrix products  123 us (22%)
  waiting for transfers between devices  60.3 us (11%)
  loops' own time  23 us (4%)
  blocking collectives  21.2 us (4%)
  other arithmetic  10.8 us (2%)
    dot_general x216, matrix products, contract(): lax.dot_general(left, right, (((left_dim,), (right_dim,)), ((), ())), pre...  122 us
    ppermute x32, starting transfers between devices, shifted(): return lax.ppermute(block, axis, route)  97.3 us
    all_to_all x2, starting transfers between devices, sum_in_two_steps(): lax.all_to_all(nearer, far, split_axis=0, concat_axis=0, tiled=True)  42.1 us
    all_to_all x2, waiting for transfers between devices, sum_in_two_steps(): lax.all_to_all(nearer, far, split_axis=0, concat_axis=0, tiled=True)  35.2 us
    all_to_all x2, starting transfers between devices, sent_to_all(): return lax.all_to_all(copies, axis, split_axis=0, concat_axis=0, tiled=True)  26.1 us
    reshape x72, local copies, waits for them, and re-layouts, skew_in(): return flat[rows - 1:rows - 1 + rows * line].reshape(rows, line)[:, :width]  24.1 us
    reshape x72, local copies, waits for them, and re-layouts, skew_out(): padded = jnp.pad(dense, ((0, 0), (0, rows - 1))).reshape(-1)  23.6 us
    another operation x1, loops' own time, body(): lax.map(every_pair, (query_heads, split_heads(key_window), split_heads(va...  23 us
  transfers between devices with their start and end apart: 37, of which 10 were waited for; matrix products, arithmetic and copies ran while one was open for 9% of the time, Pallas kernels for 0%

commit v1 on v0

v1 whole, which is shorter than its diff:
```python
import functools
import math

import jax
import jax.numpy as jnp
from jax import lax
from jax.experimental import pallas as pl
from jax.experimental.pallas import tpu as pltpu
from jax.sharding import PartitionSpec as P

HD = 64
T = 128
NY = 4
f32 = jnp.float32
bf16 = jnp.bfloat16
SCALE = 1.0 / math.sqrt(3.0 * HD)
ANY = pl.BlockSpec(memory_space=pl.ANY)
VM = pl.BlockSpec(memory_space=pltpu.VMEM)


def dot(a, b, ca=1, cb=0):
    return lax.dot_general(a, b, (((ca,), (cb,)), ((), ())), preferred_element_type=f32)


def remote(src, dst, send, recv, seq, head=None):
    where = {"seq": seq} if head is None else {"seq": seq, "head": head}
    return pltpu.make_async_remote_copy(
        src_ref=src, dst_ref=dst, send_sem=send, recv_sem=recv,
        device_id=where, device_id_type=pl.DeviceIdType.MESH,
    )


def greet(seq, head=None):
    where = {"seq": seq} if head is None else {"seq": seq, "head": head}
    pl.semaphore_signal(
        pltpu.get_barrier_semaphore(), inc=1, device_id=where,
        device_id_type=pl.DeviceIdType.MESH,
    )


def lanes(p):
    return pl.ds(pl.multiple_of(p * T, T), T)


def rows(start):
    return pl.ds(pl.multiple_of(start, T), T)


def halo_kernel(nc, q_ref, k_ref, v_ref, g_ref, rel_ref, wq_ref, wk_ref, rev_ref,
                q2_ref, g2_ref, kw_ref, vw_ref, pb_ref,
                rel_v, w_v, send, recv, local):
    s = lax.axis_index("seq")
    c, p = s // 2, lax.rem(s, 2)
    o = 1 - p
    far = [-2, 2, -1, 1]

    def chip(d):
        return lax.rem(c + d + nc, nc)

    for d in far:
        for pp in range(2):
            greet(2 * chip(d) + pp)
    greet(2 * c + o)

    loads = []

    def load(src, dst):
        copy = pltpu.make_async_copy(src, dst, local.at[len(loads)])
        copy.start()
        loads.append(copy)

    load(rel_ref, rel_v)
    load(wk_ref.at[:, lanes(p)], w_v.at[0])
    load(wq_ref.at[:, lanes(p)], w_v.at[1])
    load(k_ref.at[:, lanes(p)], kw_ref.at[rows(2 * 2 * T + T * p)])
    load(v_ref.at[:, lanes(p)], vw_ref.at[rows(2 * 2 * T + T * p)])
    load(q_ref.at[:, lanes(p)], q2_ref.at[rows(T * p)])
    load(g_ref.at[:, lanes(p)], g2_ref.at[rows(T * p)])

    pl.semaphore_wait(pltpu.get_barrier_semaphore(), 9)

    sent = []

    def push(src, dst, slot, seq):
        copy = remote(src, dst, send.at[len(sent)], recv.at[slot], seq)
        copy.start()
        sent.append(copy)

    for d in far:
        for pp in range(2):
            row = rows(2 * T * (2 - d) + T * p)
            base = ((d + 2) * 2 + p) * 2
            push(k_ref.at[:, pl.ds(pp * T, T)], kw_ref.at[row], base, 2 * chip(d) + pp)
            push(v_ref.at[:, pl.ds(pp * T, T)], vw_ref.at[row], base + 1, 2 * chip(d) + pp)
    row = rows(4 * T + T * p)
    push(k_ref.at[:, lanes(o)], kw_ref.at[row], 20, 2 * c + o)
    push(v_ref.at[:, lanes(o)], vw_ref.at[row], 21, 2 * c + o)
    push(q_ref.at[:, lanes(o)], q2_ref.at[rows(T * p)], 22, 2 * c + o)
    push(g_ref.at[:, lanes(o)], g2_ref.at[rows(T * p)], 23, 2 * c + o)

    for copy in loads[:3]:
        copy.wait()
    pos_key = dot(rel_v[...], w_v[0]).astype(bf16)
    pos_query = dot(rel_v[...], w_v[1]).astype(bf16)
    both = jnp.concatenate([pos_key, pos_query], 1)
    buckets = both.shape[0]
    column = jnp.transpose(jnp.broadcast_to(rev_ref[...], (T, rev_ref.shape[1])))
    lane = lax.broadcasted_iota(jnp.int32, column.shape, 1)
    onehot = jnp.concatenate(
        [(column == lane + T * b).astype(f32).astype(bf16) for b in range(buckets // T)], 1
    )
    pb_ref[...] = dot(onehot, both).astype(bf16)

    for copy in loads[3:]:
        copy.wait()
    for copy in sent:
        copy.wait_send()
    for d in far:
        for pp in range(2):
            row = pl.ds(2 * T * (2 - d) + T * pp, T)
            base = ((d + 2) * 2 + pp) * 2
            remote(kw_ref.at[row], kw_ref.at[row], send.at[0], recv.at[base], s).wait_recv()
            remote(vw_ref.at[row], vw_ref.at[row], send.at[0], recv.at[base + 1], s).wait_recv()
    row = rows(4 * T + T * o)
    remote(kw_ref.at[row], kw_ref.at[row], send.at[0], recv.at[20], s).wait_recv()
    remote(vw_ref.at[row], vw_ref.at[row], send.at[0], recv.at[21], s).wait_recv()
    row = rows(T * o)
    remote(q2_ref.at[row], q2_ref.at[row], send.at[0], recv.at[22], s).wait_recv()
    remote(g2_ref.at[row], g2_ref.at[row], send.at[0], recv.at[23], s).wait_recv()


def halo(q, k, v, g, rel, wq, wk, rev, nc):
    return pl.pallas_call(
        functools.partial(halo_kernel, nc),
        out_shape=(
            jax.ShapeDtypeStruct((2 * T, T), bf16),
            jax.ShapeDtypeStruct((2 * T, T), bf16),
            jax.ShapeDtypeStruct((10 * T, T), bf16),
            jax.ShapeDtypeStruct((10 * T, T), bf16),
            jax.ShapeDtypeStruct((rev.shape[1], 2 * T), bf16),
        ),
        in_specs=[ANY] * 7 + [VM],
        out_specs=(VM,) * 5,
        scratch_shapes=[
            pltpu.VMEM(rel.shape, bf16),
            pltpu.VMEM((2, wq.shape[0], T), bf16),
            pltpu.SemaphoreType.DMA((20,)),
            pltpu.SemaphoreType.DMA((24,)),
            pltpu.SemaphoreType.DMA((7,)),
        ],
        compiler_params=pltpu.CompilerParams(collective_id=0, has_side_effects=True),
        name="halo",
    )(q, k, v, g, rel, wq, wk, rev)


def attention_kernel(rb, q_ref, g_ref, kw_ref, vw_ref, pb_ref, rev_ref, len_ref,
                     dq_ref, dk_ref, dv_ref, bp_ref,
                     q2, g2, k2, pk2, pqr2, qrevt, krevt, sc, dp, dsb,
                     dqa, dka, dva, gt, ht):
    c = lax.axis_index("seq") // 2
    keys = kw_ref.shape[0]
    tiles = keys // T
    span = pb_ref.shape[0]
    ri = lax.broadcasted_iota(jnp.int32, (T, T), 0)
    ci = lax.broadcasted_iota(jnp.int32, (T, T), 1)
    flip = (ri + ci == T - 1).astype(f32).astype(bf16)

    ndocs = len_ref.shape[1]
    e = lax.broadcasted_iota(jnp.int32, (ndocs, ndocs), 1)
    d = lax.broadcasted_iota(jnp.int32, (ndocs, ndocs), 0)
    lens = jnp.broadcast_to(len_ref[...], (ndocs, ndocs))
    ends = jnp.sum(jnp.where(e <= d, lens, 0), axis=1, keepdims=True)
    shift = (c - 2) * 2 * T
    pos = lax.broadcasted_iota(jnp.int32, (ndocs, 2 * T), 1) + c * 2 * T
    first = jnp.max(jnp.where(ends <= pos, ends, 0), axis=0, keepdims=True) - shift
    last = jnp.min(jnp.where(ends > pos, ends, 1 << 30), axis=0, keepdims=True) - shift

    zero_band = jnp.zeros((2 * T, T), bf16)
    for h in range(2):
        def masked(x):
            lane = lax.broadcasted_iota(jnp.int32, x.shape, 1)
            keep = (lane < HD) if h == 0 else (lane >= HD)
            return jnp.where(keep, x, jnp.zeros_like(x))
        qh = masked(q_ref[...])
        q2[h] = qh
        g2[h] = masked(g_ref[...])
        pk2[h] = masked(pb_ref[:, :T])
        pqr2[h, : 2 * T] = zero_band
        pqr2[h, 2 * T : 2 * T + span] = masked(pb_ref[:, T:])
        pqr2[h, 2 * T + span :] = zero_band
        for r in range(2):
            qrevt[h, :, r * T : (r + 1) * T] = jnp.transpose(
                dot(flip, qh[r * T : (r + 1) * T])
            ).astype(bf16)
        for j in range(tiles):
            kh = masked(kw_ref[j * T : (j + 1) * T])
            k2[h, j * T : (j + 1) * T] = kh
            krevt[h, :, j * T : (j + 1) * T] = jnp.transpose(dot(flip, kh)).astype(bf16)
    dqa[...] = jnp.zeros_like(dqa)
    dka[...] = jnp.zeros_like(dka)
    dva[...] = jnp.zeros_like(dva)
    gt[...] = jnp.zeros_like(gt)
    ht[...] = jnp.zeros_like(ht)
    wide = 9 * T

    def head(h, carry):
        sc[...] = jnp.zeros_like(sc)
        for r in range(2):
            a = dot(q2[h, r * T : (r + 1) * T], pb_ref[:, :T], 1, 1)
            a = jnp.concatenate([a, jnp.zeros((T, wide - span), f32)], 1)
            a = pltpu.roll(a, 1, 1, stride=1, stride_axis=0)
            for j in range(9):
                sc[(r + j) * T : (r + j + 1) * T, r * T : (r + 1) * T] = jnp.transpose(
                    a[:, j * T : (j + 1) * T]
                )
        top = jnp.full((8, 2 * T), -1e30, f32)
        for j in range(tiles):
            at = slice(j * T, (j + 1) * T)
            band = slice((9 - j) * T, (9 - j) * T + 3 * T)
            b = dot(kw_ref[at], pqr2[h, band], 1, 1)
            b = pltpu.roll(b, 2 * T + 1, 1, stride=1, stride_axis=0)[:, : 2 * T]
            x = SCALE * (dot(kw_ref[at], q2[h], 1, 1) + sc[at] + b)
            at_key = lax.broadcasted_iota(jnp.int32, (T, 2 * T), 0) + j * T
            x = jnp.where((at_key >= first) & (at_key < last), x, -1e30)
            sc[at] = x
            top = jnp.maximum(top, jnp.max(x.reshape(T // 8, 8, 2 * T), axis=0))
        top = jnp.max(top, axis=0, keepdims=True)
        total = jnp.zeros((8, 2 * T), f32)
        along = jnp.zeros((8, 2 * T), f32)
        for j in range(tiles):
            at = slice(j * T, (j + 1) * T)
            x = jnp.exp(sc[at] - top)
            y = dot(vw_ref[at], g2[h], 1, 1)
            sc[at] = x
            dp[at] = y
            total = total + jnp.sum(x.reshape(T // 8, 8, 2 * T), axis=0)
            along = along + jnp.sum((x * y).reshape(T // 8, 8, 2 * T), axis=0)
        inv = 1.0 / jnp.sum(total, axis=0, keepdims=True)
        row_dot = jnp.sum(along, axis=0, keepdims=True) * inv
        for j in range(tiles):
            at = slice(j * T, (j + 1) * T)
            band = slice((9 - j) * T, (9 - j) * T + 3 * T)
            prob = sc[at] * inv
            ds = (prob * (dp[at] - row_dot)).astype(bf16)
            dsb[at] = ds
            dva[at] += dot(prob.astype(bf16), g2[h])
            back = dot(flip, ds)
            skew = jnp.concatenate([back, jnp.zeros((T, T), f32)], 1)
            skew = pltpu.roll(skew, 0, 1, stride=1, stride_axis=0).astype(bf16)
            dka[at] += dot(back.astype(bf16), q2[h]) + dot(skew, pqr2[h, band])
            ht[:, band] += dot(krevt[h, :, at], skew)
        for r in range(2):
            part = slice(r * T, (r + 1) * T)
            reach = slice(r * T, r * T + wide)
            back = dot(flip, dsb[reach, part], 1, 1)
            skew = pltpu.roll(back, span, 1, stride=1, stride_axis=0)[:, :span].astype(bf16)
            dqa[part] += dot(back.astype(bf16), k2[h, reach]) + dot(skew, pk2[h])
            gt[...] += dot(qrevt[h, :, part], skew)
        return carry

    lax.fori_loop(0, 2, head, 0)

    for r in range(2):
        part = slice(r * T, (r + 1) * T)
        dq_ref[part] = dot(flip, (SCALE * dqa[part]).astype(bf16)).astype(bf16)
    for j in range(tiles):
        at = slice(j * T, (j + 1) * T)
        dk_ref[at] = dot(flip, (SCALE * dka[at]).astype(bf16)).astype(bf16)
        dv_ref[at] = dva[at].astype(bf16)
    n = bp_ref.shape[0]
    buckets = n * rb
    number = lax.broadcasted_iota(jnp.int32, (buckets, span), 0)
    onehot = (number == rev_ref[...]).astype(f32).astype(bf16)
    bk = SCALE * dot(onehot, gt[...].astype(bf16), 1, 1)
    bq = SCALE * dot(onehot, ht[:, 2 * T : 2 * T + span].astype(bf16), 1, 1)
    bp_ref[...] = jnp.concatenate(
        [bk.reshape(n, rb, T), bq.reshape(n, rb, T)], 1
    ).astype(bf16)


def attention(q2, g2, kw, vw, pb, rev, lens, nc, buckets):
    keys, span = kw.shape[0], pb.shape[0]
    rb = buckets // nc
    return pl.pallas_call(
        functools.partial(attention_kernel, rb),
        out_shape=(
            jax.ShapeDtypeStruct((2 * T, T), bf16),
            jax.ShapeDtypeStruct((keys, T), bf16),
            jax.ShapeDtypeStruct((keys, T), bf16),
            jax.ShapeDtypeStruct((nc, 2 * rb, T), bf16),
        ),
        in_specs=[VM] * 7,
        out_specs=(VM,) * 4,
        scratch_shapes=[
            pltpu.VMEM((2, 2 * T, T), bf16),
            pltpu.VMEM((2, 2 * T, T), bf16),
            pltpu.VMEM((2, keys, T), bf16),
            pltpu.VMEM((2, span, T), bf16),
            pltpu.VMEM((2, span + 4 * T, T), bf16),
            pltpu.VMEM((2, T, 2 * T), bf16),
            pltpu.VMEM((2, T, keys), bf16),
            pltpu.VMEM((keys, 2 * T), f32),
            pltpu.VMEM((keys, 2 * T), f32),
            pltpu.VMEM((keys, 2 * T), bf16),
            pltpu.VMEM((2 * T, T), f32),
            pltpu.VMEM((keys, T), f32),
            pltpu.VMEM((keys, T), f32),
            pltpu.VMEM((T, span), f32),
            pltpu.VMEM((T, span + 4 * T), f32),
        ],
        name="attention",
    )(q2, g2, kw, vw, pb, rev, lens)


def sums_kernel(nz, ny, nx, bp_ref, dq_ref, dk_ref, dv_ref, rel_ref, wq_ref, wk_ref,
                dqo_ref, dko_ref, dvo_ref, relo_ref, wqo_ref, wko_ref,
                wv, relb, rkv, rq, yrecv, zsend, zrecv, own, ag, xpart, xrecv,
                relz, rely, relp, wtmp, wsend, wrecv, send, recv, local):
    nc = nz * ny
    s = lax.axis_index("seq")
    hx = lax.axis_index("head")
    c, p = s // 2, lax.rem(s, 2)
    o = 1 - p
    z, y = c // ny, lax.rem(c, ny)
    rb2 = bp_ref.shape[1]
    rb = rb2 // 2
    width = rel_ref.shape[1]
    dr2 = width // nc
    dr = dr2 // 2
    m = 2 * hx + p
    hops = [-2, 2, -1, 1]

    def chip(d):
        return lax.rem(c + d + nc, nc)

    def ypeer(k):
        return lax.rem(y + k, ny)

    def zpeer(k):
        return lax.rem(z + k, nz)

    def mpeer(k):
        return lax.rem(m + k, 2 * nx)

    def at(zz, yy):
        return 2 * (zz * ny + yy) + p

    yk = sorted(range(1, ny), key=lambda k: -min(k, ny - k))
    zk = sorted(range(1, nz), key=lambda k: -min(k, nz - k))
    mk = range(1, 2 * nx)
    mate = 2 * c + o

    for k in zk:
        greet(at(zpeer(k), y))
    for k in yk:
        greet(at(z, ypeer(k)))
    for d in hops:
        for pp in range(2):
            greet(2 * chip(d) + pp)
    for k in mk:
        greet(2 * c + lax.rem(mpeer(k), 2), mpeer(k) // 2)
    greet(mate)

    loads = []

    def load(src, dst):
        copy = pltpu.make_async_copy(src, dst, local.at[len(loads)])
        copy.start()
        loads.append(copy)

    load(wk_ref.at[:, lanes(p)], wv.at[0])
    load(wq_ref.at[:, lanes(p)], wv.at[1])
    load(rel_ref.at[:, lanes(c * dr2 // T)], relb)
    load(dk_ref.at[rows(4 * T + p * T)], rkv.at[2, p, 0])
    load(dv_ref.at[rows(4 * T + p * T)], rkv.at[2, p, 1])
    load(dq_ref.at[rows(p * T)], rq.at[p])

    pl.semaphore_wait(
        pltpu.get_barrier_semaphore(), len(zk) + len(yk) + 8 + len(mk) + 1
    )

    sent = []
    slots = [0]

    def push(src, dst, slot, seq, head=None):
        copy = remote(src, dst, send.at[len(sent)], recv.at[slot], seq, head)
        copy.start()
        sent.append(copy)

    def take(count):
        base = slots[0]
        slots[0] += count
        return base

    def arrive(dst, slot):
        remote(dst, dst, send.at[0], recv.at[slot], s).wait_recv()

    ys = take(ny)
    for k in yk:
        push(bp_ref.at[pl.ds(nz * ypeer(k), nz)], yrecv.at[k - 1], ys + k - 1, at(z, ypeer(k)))

    rs = take(20)
    qs = take(1)
    for d in hops:
        for pp in range(2):
            row = pl.ds(2 * T * (d + 2) + T * pp, T)
            slot = rs + ((d + 2) * 2 + p) * 2
            push(dk_ref.at[row], rkv.at[d + 2, p, 0], slot, 2 * chip(d) + pp)
            push(dv_ref.at[row], rkv.at[d + 2, p, 1], slot + 1, 2 * chip(d) + pp)
    slot = rs + (2 * 2 + p) * 2
    push(dk_ref.at[rows(4 * T + T * o)], rkv.at[2, p, 0], slot, mate)
    push(dv_ref.at[rows(4 * T + T * o)], rkv.at[2, p, 1], slot + 1, mate)
    push(dq_ref.at[rows(T * o)], rq.at[p], qs, mate)

    part = bp_ref[pl.ds(nz * y, nz)].astype(f32)
    for k in yk:
        arrive(yrecv.at[k - 1], ys + k - 1)
    for k in yk:
        part = part + yrecv[k - 1].astype(f32)
    zsend[...] = part.astype(bf16)

    zs = take(nz)
    for k in zk:
        push(zsend.at[zpeer(k)], zrecv.at[k - 1], zs + k - 1, at(zpeer(k), y))
    for copy in loads:
        copy.wait()
    part = zsend[z].astype(f32)
    for k in reversed(zk):
        arrive(zrecv.at[k - 1], zs + k - 1)
        part = part + zrecv[k - 1].astype(f32)
    low = part.astype(bf16)
    own[...] = low
    ag[nz * y + z] = low

    gs = take(nz)
    for k in zk:
        push(own, ag.at[nz * y + z], gs + k - 1, at(zpeer(k), y))

    both = part.astype(bf16).astype(f32)
    rel_part = dot(both[:rb].astype(bf16), wv[0], 1, 1) + dot(both[rb:].astype(bf16), wv[1], 1, 1)
    for i in range(2 * nx):
        xpart[i] = rel_part[:, i * T : (i + 1) * T]
    xs = take(2 * nx)
    for k in mk:
        push(xpart.at[mpeer(k)], xrecv.at[k - 1], xs + k - 1,
             2 * c + lax.rem(mpeer(k), 2), mpeer(k) // 2)
    total = xpart[m]
    for k in mk:
        arrive(xrecv.at[k - 1], xs + k - 1)
        total = total + xrecv[k - 1]
    relz[z] = total
    ls = take(nz)
    for k in zk:
        push(xsum_src(relz, z), relz.at[z], ls + k - 1, at(zpeer(k), y))

    for k in reversed(zk):
        arrive(ag.at[nz * y + zpeer(nz - k)], gs + k - 1)
    hs = take(ny)
    mine = pl.ds(nz * y, nz)
    for k in yk:
        push(ag.at[mine], ag.at[mine], hs + k - 1, at(z, ypeer(k)))
    for k in reversed(zk):
        arrive(relz.at[zpeer(nz - k)], ls + k - 1)
    rely[y] = relz[...].reshape(nz * rb, T).astype(bf16)
    ms = take(ny)
    es = take(ny)
    for k in yk:
        push(rely.at[y], rely.at[y], ms + k - 1, at(z, ypeer(k)))
    push(rely.at[y], relp.at[y], es, mate)

    for d in (-2, -1, 0, 1, 2):
        for pp in range(2):
            if d != 0:
                arrive(rkv.at[d + 2, pp, 0], rs + ((d + 2) * 2 + pp) * 2)
                arrive(rkv.at[d + 2, pp, 1], rs + ((d + 2) * 2 + pp) * 2 + 1)
    arrive(rkv.at[2, o, 0], rs + (2 * 2 + o) * 2)
    arrive(rkv.at[2, o, 1], rs + (2 * 2 + o) * 2 + 1)
    arrive(rq.at[o], qs)
    for pp in range(2):
        col = slice(pp * T, (pp + 1) * T)
        dqo_ref[:, col] = rq[pp]
        for i, out in ((0, dko_ref), (1, dvo_ref)):
            x = rkv[0, pp, i].astype(f32)
            for d in range(1, 5):
                x = x + rkv[d, pp, i].astype(f32)
            out[:, col] = x.astype(bf16)

    for k in reversed(yk):
        arrive(ag.at[pl.ds(nz * ypeer(ny - k), nz)], hs + k - 1)
    every = ag[...].astype(f32)
    for i in range(2):
        grad = every[:, i * rb : (i + 1) * rb].reshape(nc * rb, T).astype(bf16)
        wtmp[i] = dot(relb[...], grad, 0, 0)
    first = lax.rem(c * dr2, T)
    theirs = pl.ds(pl.multiple_of(first + dr * o, dr), dr)
    ours = pl.ds(pl.multiple_of(first + dr * p, dr), dr)
    wsend[...] = wtmp[:, theirs]
    ws = take(1)
    push(wsend, wrecv, ws, mate)
    wko_ref[:, lanes(p)] = wtmp[0, ours]
    wqo_ref[:, lanes(p)] = wtmp[1, ours]

    for k in reversed(yk):
        arrive(rely.at[ypeer(ny - k)], ms + k - 1)
        push(rely.at[ypeer(ny - k)], relp.at[ypeer(ny - k)], es + k, mate)
    relo_ref[:, lanes(p)] = rely[...].reshape(nc * rb, T).astype(f32)
    arrive(wrecv, ws)
    wko_ref[:, lanes(o)] = wrecv[0]
    wqo_ref[:, lanes(o)] = wrecv[1]
    arrive(relp.at[y], es)
    for k in reversed(yk):
        arrive(relp.at[ypeer(ny - k)], es + k)
    relo_ref[:, lanes(o)] = relp[...].reshape(nc * rb, T).astype(f32)
    for copy in sent:
        copy.wait_send()


def xsum_src(ref, z):
    return ref.at[z]


def sums(bp, dq, dk, dv, rel, wq, wk, nz, ny, nx):
    nc = nz * ny
    buckets, width = rel.shape
    rb = buckets // nc
    dr = width // nc // 2
    return pl.pallas_call(
        functools.partial(sums_kernel, nz, ny, nx),
        out_shape=(
            jax.ShapeDtypeStruct((T, 2 * T), bf16),
            jax.ShapeDtypeStruct((T, 2 * T), bf16),
            jax.ShapeDtypeStruct((T, 2 * T), bf16),
            jax.ShapeDtypeStruct((buckets, 2 * T), f32),
            jax.ShapeDtypeStruct((dr, 2 * T), f32),
            jax.ShapeDtypeStruct((dr, 2 * T), f32),
        ),
        in_specs=[VM] + [ANY] * 6,
        out_specs=(VM,) * 6,
        scratch_shapes=[
            pltpu.VMEM((2, width, T), bf16),
            pltpu.VMEM((buckets, T), bf16),
            pltpu.VMEM((5, 2, 2, T, T), bf16),
            pltpu.VMEM((2, T, T), bf16),
            pltpu.VMEM((ny, nz, 2 * rb, T), bf16),
            pltpu.VMEM((nz, 2 * rb, T), bf16),
            pltpu.VMEM((nz, 2 * rb, T), bf16),
            pltpu.VMEM((2 * rb, T), bf16),
            pltpu.VMEM((nc, 2 * rb, T), bf16),
            pltpu.VMEM((2 * nx, rb, T), f32),
            pltpu.VMEM((2 * nx, rb, T), f32),
            pltpu.VMEM((nz, rb, T), f32),
            pltpu.VMEM((ny, nz * rb, T), bf16),
            pltpu.VMEM((ny, nz * rb, T), bf16),
            pltpu.VMEM((2, T, T), f32),
            pltpu.VMEM((2, dr, T), f32),
            pltpu.VMEM((2, dr, T), f32),
            pltpu.SemaphoreType.DMA((128,)),
            pltpu.SemaphoreType.DMA((128,)),
            pltpu.SemaphoreType.DMA((6,)),
        ],
        compiler_params=pltpu.CompilerParams(collective_id=1, has_side_effects=True),
        name="sums",
    )(bp, dq, dk, dv, rel, wq, wk)


def body(ny, queries, keys, values, out_grad, rel_emb, w_query, w_key, doc_lengths, bucket_table):
    nc = lax.axis_size("seq") // 2
    nx = lax.axis_size("head")
    rev = jnp.flip(bucket_table).reshape(1, -1)
    lens = doc_lengths.reshape(1, -1)
    q2, g2, kw, vw, pb = halo(queries, keys, values, out_grad, rel_emb, w_query, w_key, rev, nc)
    dq, dk, dv, bp = attention(q2, g2, kw, vw, pb, rev, lens, nc, rel_emb.shape[0])
    query_grad, key_grad, value_grad, rel_grad, wq_grad, wk_grad = sums(
        bp, dq, dk, dv, rel_emb, w_query, w_key, nc // ny, ny, nx
    )
    return (query_grad, key_grad, value_grad, rel_grad, wq_grad, wk_grad)


def solution(mesh, ny=NY):
    shard = P("seq", "head")
    return jax.shard_map(
        functools.partial(body, ny),
        mesh=mesh,
        in_specs=(shard,) * 4 + (P(), P(None, "head"), P(None, "head"), P(), P()),
        out_specs=(shard, shard, shard, P(None, "head"), shard, shard),
        check_vma=False,
    )
```

time: 550 us -> 99.5 us (0.18); the launches traced: 542 us -> 99.1 us
  starting transfers between devices: 170 us -> 0 us
  local copies, waits for them, and re-layouts: 132 us -> 7.53 us
  matrix products: 123 us -> 0 us
  Pallas kernels: 0 us -> 90.9 us
  waiting for transfers between devices: 60.3 us -> 0 us
  loops' own time: 23 us -> 0 us
  blocking collectives: 21.2 us -> 0 us
  other arithmetic: 10.8 us -> 0 us
    dot_general x218 -> x0, matrix products: 123 us -> none  [the longest x216 122 us: contract(): lax.dot_general(left, right, (((left_dim,), (right_dim,)), ((), ())), pre...]
    ppermute x32 -> x0, starting transfers between devices: 97.3 us -> none  [shifted(): return lax.ppermute(block, axis, route)]
    pallas_call x0 -> x3, Pallas kernels: none -> 90.9 us  [the longest x1 51.1 us: sums(): pl.pallas_call(functools.partial(sums_kernel, nz, ny, nx), out_shape=(jax...]
    all_to_all x5 -> x0, starting transfers between devices: 72.4 us -> none  [the longest x2 42.1 us: sum_in_two_steps(): lax.all_to_all(nearer, far, split_axis=0, concat_axis=0, tiled=True)]
    reshape x219 -> x0, local copies, waits for them, and re-layouts: 52 us -> none  [the longest x72 24.1 us: skew_in(): return flat[rows - 1:rows - 1 + rows * line].reshape(rows, line)[:, :width]]
    all_to_all x5 -> x0, waiting for transfers between devices: 43.2 us -> none  [the longest x2 35.2 us: sum_in_two_steps(): lax.all_to_all(nearer, far, split_axis=0, concat_axis=0, tiled=True)]
    another operation x1 -> x0, loops' own time: 23 us -> none  [body(): lax.map(every_pair, (query_heads, split_heads(key_window), split_heads(va...]
    while x368 -> x0, local copies, waits for them, and re-layouts: 22.5 us -> none
  transfers between devices with their start and end apart: 37 -> 0, of which waited for: 10 -> 0; matrix products, arithmetic and copies ran while one was open for 9% -> 0% of each run, Pallas kernels for 0% -> 0%
where the time goes in v1:
time: 99.5 us; the launch traced here: 99.1 us
  Pallas kernels  90.9 us (91%)
  local copies, waits for them, and re-layouts  7.53 us (8%)
    pallas_call x1, Pallas kernels, sums(): pl.pallas_call(functools.partial(sums_kernel, nz, ny, nx), out_shape=(jax...  51.1 us
    pallas_call x1, Pallas kernels, halo(): pl.pallas_call(functools.partial(halo_kernel, nc), out_shape=(jax.ShapeDt...  24.1 us
    pallas_call x1, Pallas kernels, attention(): pl.pallas_call(functools.partial(attention_kernel, rb), out_shape=(jax.Sh...  15.7 us
    unnamed x14, local copies, waits for them, and re-layouts  6.18 us

profile of v1, /device:TPU:1, one launch (start us, length us, event | category | flops | bytes accessed | tf_op | source)
XLA Modules:
  0.0 99.1 jit_solution(12513319178117259560)
XLA Ops:
  0.6 1.4 %rev.4 = s32[1024]{0:T(1024)} reverse(s32[1024]{0:T(1024)} %param.17), dimensions={0} | reverse | bytes 8192 | tf_op jit(solution)/shard_map/jit(_flip)/rev | solution.py:569
  2.0 24.1 %halo.1 = (bf16[256,128]{1,0:T(8,128)(2,1)}, bf16[256,128]{1,0:T(8,128)(2,1)}, bf16[1280,128]{1,0:T(8,128)(2,1)}, bf16[1280,128]{1,0:T(8,128)(2,1)}, bf16[1024,256]{1,0:T(8,128)(2,1)}) custom-call(bf16[128,256]{1,0:T(8,128)(2,1)} %q_ref.1, bf16[128,256]{1,0:T(8,128)(2,1)} %k_ref.1, bf16[128,256]{1,0:T(8,128)(2,1)} %v_ref.1, bf16[128,256]{1,0:T(8,128)(2,1)} %g_ref.1, ...), custom_call_target="tpu_custom_call" | custom-call | tf_op jit(solution)/shard_map/halo/pallas_call | solution.py:133
  26.0 15.7 %attention.1 = (bf16[256,128]{1,0:T(8,128)(2,1)}, bf16[1280,128]{1,0:T(8,128)(2,1)}, bf16[1280,128]{1,0:T(8,128)(2,1)}, bf16[64,16,128]{2,1,0:T(8,128)(2,1)}) custom-call(bf16[256,128]{1,0:T(8,128)(2,1)} %get-tuple-element.15.q_ref, bf16[256,128]{1,0:T(8,128)(2,1)} %get-tuple-element.16.g_ref, bf16[1280,128]{1,0:T(8,128)(2,1)} %get-tuple-element.17.kw_ref, ...), custom_call_target="tpu_custom_call" | custom-call | tf_op jit(solution)/shard_map/attention/pallas_call | solution.py:284
  41.7 51.1 %sums.1 = (bf16[128,256]{1,0:T(8,128)(2,1)}, bf16[128,256]{1,0:T(8,128)(2,1)}, bf16[128,256]{1,0:T(8,128)(2,1)}, f32[512,256]{1,0:T(8,128)}, f32[8,256]{1,0:T(8,128)}, /*index=5*/f32[8,256]{1,0:T(8,128)}) custom-call(bf16[64,16,128]{2,1,0:T(8,128)(2,1)} %get-tuple-element.20.bp_ref, bf16[256,128]{1,0:T(8,128)(2,1)} %get-tuple-element.21.dq_ref, ...), custom_call_target="tpu_custom_call" | custom-call | tf_op jit(solution)/shard_map/sums/pallas_call | solution.py:527
  92.9 0.0 copy-start.1
  92.9 1.5 %copy.21 = bf16[128,256]{1,0:T(8,128)(2,1)} copy(bf16[128,256]{1,0:T(8,128)(2,1)} %get-tuple-element.30) | data formatting | bytes 131072
  94.4 0.0 copy-done.1
  94.4 0.0 copy-start
  94.4 0.6 copy.22
  95.0 0.2 copy-done
  95.3 0.6 copy.23
  95.9 0.0 copy-start.3
  95.9 1.9 %copy.24 = f32[512,256]{1,0:T(8,128)} copy(f32[512,256]{1,0:T(8,128)} %get-tuple-element.33) | data formatting | bytes 1048576
  97.8 0.0 copy-done.3
  97.8 0.0 copy-start.2
  97.8 0.6 copy.25
  98.4 0.1 copy-done.2
  98.5 0.6 copy.26
Async XLA Ops:
  92.9 1.5 %copy-start.1 = (bf16[128,256]{1,0:T(8,128)(2,1)S(1)}, bf16[128,256]{1,0:T(8,128)(2,1)}, u32[]{:S(2)}) copy-start(bf16[128,256]{1,0:T(8,128)(2,1)} %get-tuple-element.31) | copy-start | bytes 196612
  94.4 0.9 copy-start
  95.9 1.9 %copy-start.3 = (f32[8,256]{1,0:T(8,128)S(1)}, f32[8,256]{1,0:T(8,128)}, u32[]{:S(2)}) copy-start(f32[8,256]{1,0:T(8,128)} %get-tuple-element.34) | copy-start | bytes 24580
  97.8 0.7 copy-start.2

commit v2 on v1

v2 whole, which is shorter than its diff:
```python
import functools
import math

import jax
import jax.numpy as jnp
from jax import lax
from jax.experimental import pallas as pl
from jax.experimental.pallas import tpu as pltpu
from jax.sharding import PartitionSpec as P

HD = 64
T = 128
NY = 4
HALO = 2
TILES = 2 * (2 * HALO + 1)
WIDE = 9 * T
f32 = jnp.float32
bf16 = jnp.bfloat16
SCALE = 1.0 / math.sqrt(3.0 * HD)
ANY = pl.BlockSpec(memory_space=pl.ANY)
VM = pl.BlockSpec(memory_space=pltpu.VMEM)


def dot(a, b, ca=1, cb=0):
    return lax.dot_general(a, b, (((ca,), (cb,)), ((), ())), preferred_element_type=f32)


def remote(src, dst, send, recv, seq, head=None):
    where = {"seq": seq} if head is None else {"seq": seq, "head": head}
    return pltpu.make_async_remote_copy(
        src_ref=src, dst_ref=dst, send_sem=send, recv_sem=recv,
        device_id=where, device_id_type=pl.DeviceIdType.MESH,
    )


def greet(seq, head=None):
    where = {"seq": seq} if head is None else {"seq": seq, "head": head}
    pl.semaphore_signal(
        pltpu.get_barrier_semaphore(), inc=1, device_id=where,
        device_id_type=pl.DeviceIdType.MESH,
    )


def lanes(p):
    return pl.ds(pl.multiple_of(p * T, T), T)


def rows(start):
    return pl.ds(pl.multiple_of(start, T), T)


def tile(j):
    return slice(j * T, (j + 1) * T)


def skewed(x, first):
    return pltpu.roll(x, first, 1, stride=1, stride_axis=0)


def head_only(x, h):
    lane = lax.broadcasted_iota(jnp.int32, x.shape, 1)
    return jnp.where((lane < HD) if h == 0 else (lane >= HD), x, jnp.zeros_like(x))


def indicator(match):
    return match.astype(f32).astype(bf16)


def whole_kernel(
    nz, ny, nx,
    q_ref, k_ref, v_ref, g_ref, rel_ref, wq_ref, wk_ref, tab_ref, len_ref,
    dqo, dko, dvo, relo, relq, wko, wqo,
    rel_v, wv, qw, gw, kw, vw, pb, oht, q2, g2, k2, pqr, qrt, krt,
    sc, dp, prb, dsb, dsr, skb, dsa, ska, dkb, dvb, dqb, gt, ht,
    bp, rkv, rq, yrecv, zsend, zrecv, own, ag, xpart, xrecv, relz,
    wtmp, wsend, wrecv, send, recv, local,
):
    nc = nz * ny
    s = lax.axis_index("seq")
    hx = lax.axis_index("head")
    c, p = s // 2, lax.rem(s, 2)
    o = 1 - p
    mate = 2 * c + o
    z, y = c // ny, lax.rem(c, ny)
    m = 2 * hx + p
    buckets, width = rel_ref.shape
    span = tab_ref.shape[1]
    rb = buckets // nc
    dr2 = width // nc
    dr = dr2 // 2
    hops = [-1, 1, -2, 2]

    def chip(d):
        return lax.rem(c + d + nc, nc)

    def ypeer(k):
        return lax.rem(y + k, ny)

    def zpeer(k):
        return lax.rem(z + k, nz)

    def mpeer(k):
        return lax.rem(m + k, 2 * nx)

    def at(zz, yy):
        return 2 * (zz * ny + yy) + p

    yk = sorted(range(1, ny), key=lambda k: -min(k, ny - k))
    zk = sorted(range(1, nz), key=lambda k: -min(k, nz - k))
    mk = range(1, 2 * nx)

    for k in zk:
        greet(at(zpeer(k), y))
    for k in yk:
        greet(at(z, ypeer(k)))
    for d in hops:
        for pp in range(2):
            greet(2 * chip(d) + pp)
    for k in mk:
        greet(2 * c + lax.rem(mpeer(k), 2), mpeer(k) // 2)
    greet(mate)

    loads = []

    def load(src, dst):
        copy = pltpu.make_async_copy(src, dst, local.at[len(loads)])
        copy.start()
        loads.append(copy)

    load(rel_ref, rel_v)
    load(wk_ref.at[:, lanes(p)], wv.at[0])
    load(wq_ref.at[:, lanes(p)], wv.at[1])
    load(k_ref.at[:, lanes(p)], kw.at[rows(2 * HALO * T + T * p)])
    load(v_ref.at[:, lanes(p)], vw.at[rows(2 * HALO * T + T * p)])
    load(q_ref.at[:, lanes(p)], qw.at[rows(T * p)])
    load(g_ref.at[:, lanes(p)], gw.at[rows(T * p)])

    ri = lax.broadcasted_iota(jnp.int32, (T, T), 0)
    ci = lax.broadcasted_iota(jnp.int32, (T, T), 1)
    flip = indicator(ri + ci == T - 1)
    table = jnp.broadcast_to(tab_ref[...], (8, span))
    high = table // 256
    low = (table - 256 * high).astype(f32).astype(bf16)
    high = high.astype(f32).astype(bf16)
    blocks = span // T
    rev = jnp.concatenate(
        [
            256.0 * dot(high[:, tile(blocks - 1 - b)], flip) + dot(low[:, tile(blocks - 1 - b)], flip)
            for b in range(blocks)
        ],
        1,
    )[:1]
    number = lax.broadcasted_iota(jnp.int32, (T, span), 0).astype(f32)
    for b in range(buckets // T):
        oht[tile(b)] = indicator(number + float(b * T) == rev)
    column = jnp.transpose(jnp.broadcast_to(rev, (T, span)))
    lane = lax.broadcasted_iota(jnp.int32, column.shape, 1).astype(f32)
    onehot = jnp.concatenate(
        [indicator(column == lane + float(T * b)) for b in range(buckets // T)], 1
    )

    ndocs = len_ref.shape[1]
    de = lax.broadcasted_iota(jnp.int32, (ndocs, ndocs), 1)
    dd = lax.broadcasted_iota(jnp.int32, (ndocs, ndocs), 0)
    lens = jnp.broadcast_to(len_ref[...], (ndocs, ndocs))
    ends = jnp.sum(jnp.where(de <= dd, lens, 0), axis=1, keepdims=True)
    shift = (c - HALO) * 2 * T
    pos = lax.broadcasted_iota(jnp.int32, (ndocs, 2 * T), 1) + c * 2 * T
    first = jnp.max(jnp.where(ends <= pos, ends, 0), axis=0, keepdims=True) - shift
    last = jnp.min(jnp.where(ends > pos, ends, 1 << 30), axis=0, keepdims=True) - shift

    for copy in loads[:3]:
        copy.wait()
    pos_key = dot(rel_v[...], wv[0]).astype(bf16)
    pos_query = dot(rel_v[...], wv[1]).astype(bf16)
    pb[...] = dot(onehot, jnp.concatenate([pos_key, pos_query], 1)).astype(bf16)
    for h in range(2):
        pqr[h, : 2 * T] = jnp.zeros((2 * T, T), bf16)
        pqr[h, 2 * T : 2 * T + span] = head_only(pb[:, T:], h)
        pqr[h, 2 * T + span :] = jnp.zeros((2 * T, T), bf16)
    ht[...] = jnp.zeros_like(ht)

    pl.semaphore_wait(
        pltpu.get_barrier_semaphore(), len(zk) + len(yk) + 8 + len(mk) + 1
    )

    sent = []
    slots = [0]

    def push(src, dst, slot, seq, head=None):
        copy = remote(src, dst, send.at[len(sent)], recv.at[slot], seq, head)
        copy.start()
        sent.append(copy)

    def take(count):
        base = slots[0]
        slots[0] += count
        return base

    def arrive(dst, slot):
        remote(dst, dst, send.at[0], recv.at[slot], s).wait_recv()

    near = take(4)
    hs = take(20)
    row = rows(T * p)
    push(q_ref.at[:, lanes(o)], qw.at[row], near, mate)
    push(g_ref.at[:, lanes(o)], gw.at[row], near + 1, mate)
    row = rows(2 * HALO * T + T * p)
    push(k_ref.at[:, lanes(o)], kw.at[row], near + 2, mate)
    push(v_ref.at[:, lanes(o)], vw.at[row], near + 3, mate)
    for d in hops:
        for pp in range(2):
            row = rows(2 * T * (HALO - d) + T * p)
            base = hs + ((d + HALO) * 2 + p) * 2
            push(k_ref.at[:, pl.ds(pp * T, T)], kw.at[row], base, 2 * chip(d) + pp)
            push(v_ref.at[:, pl.ds(pp * T, T)], vw.at[row], base + 1, 2 * chip(d) + pp)
    for copy in loads[3:]:
        copy.wait()
    arrive(qw.at[rows(T * o)], near)
    arrive(gw.at[rows(T * o)], near + 1)

    for h in range(2):
        q2[h] = head_only(qw[...], h)
        g2[h] = head_only(gw[...], h)
    for r in range(2):
        qrt[:, tile(r)] = jnp.transpose(dot(flip, qw[tile(r)])).astype(bf16)
    for h in range(2):
        sc[h, WIDE:, :T] = jnp.zeros((T, T), f32)
        sc[h, :T, T:] = jnp.zeros((T, T), f32)
        for r in range(2):
            a = dot(q2[h, tile(r)], pb[:, :T], 1, 1)
            a = skewed(jnp.concatenate([a, jnp.zeros((T, WIDE - span), f32)], 1), 1)
            for j in range(9):
                sc[h, tile(r + j), tile(r)] = jnp.transpose(a[:, tile(j)])

    arrive(kw.at[rows(2 * HALO * T + T * o)], near + 2)
    arrive(vw.at[rows(2 * HALO * T + T * o)], near + 3)

    top = [jnp.full((8, 2 * T), -1e30, f32) for _ in range(2)]

    def band(j):
        return slice((9 - j) * T, (9 - j) * T + 3 * T)

    def fold(x, op):
        return op(x.reshape(T // 8, 8, 2 * T), axis=0)

    def score(j):
        kt = kw[tile(j)]
        krt[:, tile(j)] = jnp.transpose(dot(flip, kt)).astype(bf16)
        key = lax.broadcasted_iota(jnp.int32, (T, 2 * T), 0) + j * T
        keep = (key >= first) & (key < last)
        for h in range(2):
            k2[h, tile(j)] = head_only(kt, h)
            b = skewed(dot(kt, pqr[h, band(j)], 1, 1), 2 * T + 1)[:, : 2 * T]
            x = SCALE * (dot(kt, q2[h], 1, 1) + sc[h, tile(j)] + b)
            x = jnp.where(keep, x, -1e30)
            sc[h, tile(j)] = x
            top[h] = jnp.maximum(top[h], fold(x, jnp.max))
            dp[h, tile(j)] = dot(vw[tile(j)], g2[h], 1, 1)

    score(4)
    score(5)
    for d in (-1, 1, -2, 2):
        for pp in range(2):
            j = 2 * (HALO - (-d)) + pp
            base = hs + ((-d + HALO) * 2 + pp) * 2
            arrive(kw.at[tile(j)], base)
            arrive(vw.at[tile(j)], base + 1)
        score(2 * (HALO + d))
        score(2 * (HALO + d) + 1)

    for h in range(2):
        high_score = jnp.max(top[h], axis=0, keepdims=True)
        total = jnp.zeros((8, 2 * T), f32)
        along = jnp.zeros((8, 2 * T), f32)
        for j in range(TILES):
            x = jnp.exp(sc[h, tile(j)] - high_score)
            sc[h, tile(j)] = x
            total = total + fold(x, jnp.sum)
            along = along + fold(x * dp[h, tile(j)], jnp.sum)
        inv = 1.0 / jnp.sum(total, axis=0, keepdims=True)
        row_dot = jnp.sum(along, axis=0, keepdims=True) * inv
        half = slice(h * HD, (h + 1) * HD)
        for j in range(TILES):
            prob = sc[h, tile(j)] * inv
            ds = (prob * (dp[h, tile(j)] - row_dot)).astype(bf16)
            prb[h, tile(j)] = prob.astype(bf16)
            dsb[h, tile(j)] = ds
            back = dot(flip, ds)
            dsr[h, tile(j)] = back.astype(bf16)
            skew = skewed(jnp.concatenate([back, jnp.zeros((T, T), f32)], 1), 0).astype(bf16)
            skb[h, tile(j)] = skew
            ht[half, band(j)] += dot(krt[half, tile(j)], skew)
        for r in range(2):
            back = dot(flip, dsb[h, r * T : r * T + WIDE, tile(r)], 1, 1)
            dsa[h, tile(r)] = back.astype(bf16)
            skew = skewed(back, span)[:, :span].astype(bf16)
            ska[h, tile(r)] = skew
            part = dot(qrt[half, tile(r)], skew)
            if r == 0:
                gt[half] = part
            else:
                gt[half] += part

    bk = SCALE * dot(oht[...], gt[...].astype(bf16), 1, 1)
    bq = SCALE * dot(oht[...], ht[:, 2 * T : 2 * T + span].astype(bf16), 1, 1)
    bp[...] = jnp.concatenate([bk.reshape(nc, rb, T), bq.reshape(nc, rb, T)], 1).astype(bf16)

    ys = take(ny)
    for k in yk:
        push(bp.at[pl.ds(nz * ypeer(k), nz)], yrecv.at[k - 1], ys + k - 1, at(z, ypeer(k)))

    for j in (0, 1, 8, 9, 2, 3, 6, 7, 4, 5):
        dv = dot(prb[0, tile(j)], g2[0]) + dot(prb[1, tile(j)], g2[1])
        dvb[tile(j)] = dv.astype(bf16)
        dk = dot(dsr[0, tile(j)], q2[0]) + dot(dsr[1, tile(j)], q2[1])
        dk = dk + dot(skb[0, tile(j)], pqr[0, band(j)]) + dot(skb[1, tile(j)], pqr[1, band(j)])
        dkb[tile(j)] = dot(flip, (SCALE * dk).astype(bf16)).astype(bf16)
    for r in range(2):
        reach = slice(r * T, r * T + WIDE)
        dq = dot(dsa[0, tile(r)], k2[0, reach]) + dot(dsa[1, tile(r)], k2[1, reach])
        for h in range(2):
            dq = dq + head_only(dot(ska[h, tile(r)], pb[:, :T]), h)
        dqb[tile(r)] = dot(flip, (SCALE * dq).astype(bf16)).astype(bf16)

    part = bp[pl.ds(nz * y, nz)].astype(f32)
    for k in yk:
        arrive(yrecv.at[k - 1], ys + k - 1)
    for k in yk:
        part = part + yrecv[k - 1].astype(f32)
    zsend[...] = part.astype(bf16)

    zs = take(nz)
    for k in zk:
        push(zsend.at[zpeer(k)], zrecv.at[k - 1], zs + k - 1, at(zpeer(k), y))

    rs = take(20)
    qs = take(1)
    for d in hops:
        for pp in range(2):
            row = tile(2 * (d + HALO) + pp)
            slot = rs + ((d + HALO) * 2 + p) * 2
            push(dkb.at[row], rkv.at[d + HALO, p, 0], slot, 2 * chip(d) + pp)
            push(dvb.at[row], rkv.at[d + HALO, p, 1], slot + 1, 2 * chip(d) + pp)
    row = rows(2 * HALO * T + T * o)
    slot = rs + (HALO * 2 + p) * 2
    push(dkb.at[row], rkv.at[HALO, p, 0], slot, mate)
    push(dvb.at[row], rkv.at[HALO, p, 1], slot + 1, mate)
    push(dqb.at[rows(T * o)], rq, qs, mate)

    part = zsend[z].astype(f32)
    for k in reversed(zk):
        arrive(zrecv.at[k - 1], zs + k - 1)
        part = part + zrecv[k - 1].astype(f32)
    low = part.astype(bf16)
    own[...] = low
    ag[nz * y + z] = low

    gs = take(nz)
    for k in zk:
        push(own, ag.at[nz * y + z], gs + k - 1, at(zpeer(k), y))

    both = low.astype(f32)
    rel_part = dot(both[:rb].astype(bf16), wv[0], 1, 1) + dot(both[rb:].astype(bf16), wv[1], 1, 1)
    for i in range(2 * nx):
        xpart[i] = rel_part[:, tile(i)]
    xs = take(2 * nx)
    for k in mk:
        push(xpart.at[mpeer(k)], xrecv.at[k - 1], xs + k - 1,
             2 * c + lax.rem(mpeer(k), 2), mpeer(k) // 2)
    total = xpart[m]
    for k in mk:
        arrive(xrecv.at[k - 1], xs + k - 1)
        total = total + xrecv[k - 1]
    relz[z] = total
    ls = take(nz)
    for k in zk:
        push(relz.at[z], relz.at[z], ls + k - 1, at(zpeer(k), y))

    for k in reversed(zk):
        arrive(ag.at[nz * y + zpeer(nz - k)], gs + k - 1)
    us = take(ny)
    mine = pl.ds(nz * y, nz)
    for k in yk:
        push(ag.at[mine], ag.at[mine], us + k - 1, at(z, ypeer(k)))

    dqo[:, lanes(p)] = dqb[rows(T * p)]
    arrive(rq, qs)
    dqo[:, lanes(o)] = rq[...]
    row = rows(2 * HALO * T + T * p)
    rkv[HALO, p, 0] = dkb[row]
    rkv[HALO, p, 1] = dvb[row]
    arrive(rkv.at[HALO, o, 0], rs + (HALO * 2 + o) * 2)
    arrive(rkv.at[HALO, o, 1], rs + (HALO * 2 + o) * 2 + 1)
    for d in hops:
        for pp in range(2):
            arrive(rkv.at[d + HALO, pp, 0], rs + ((d + HALO) * 2 + pp) * 2)
            arrive(rkv.at[d + HALO, pp, 1], rs + ((d + HALO) * 2 + pp) * 2 + 1)
    for pp in range(2):
        for i, out in ((0, dko), (1, dvo)):
            x = rkv[0, pp, i].astype(f32)
            for d in range(1, 2 * HALO + 1):
                x = x + rkv[d, pp, i].astype(f32)
            out[:, tile(pp)] = x.astype(bf16)

    for k in reversed(zk):
        arrive(relz.at[zpeer(nz - k)], ls + k - 1)
    relo[y] = relz[...].reshape(nz * rb, T).astype(bf16)
    ms = take(ny)
    es = take(ny)
    for k in yk:
        push(relo.at[y], relo.at[y], ms + k - 1, at(z, ypeer(k)))
    push(relo.at[y], relq.at[y], es, mate)

    for k in reversed(yk):
        arrive(ag.at[pl.ds(nz * ypeer(ny - k), nz)], us + k - 1)
    every = ag[...].astype(f32)
    for i in range(2):
        grad = every[:, i * rb : (i + 1) * rb].reshape(buckets, T).astype(bf16)
        wtmp[i] = dot(rel_v[:, lanes(c * dr2 // T)], grad, 0, 0)
    start = lax.rem(c * dr2, T)
    wsend[...] = wtmp[:, pl.ds(pl.multiple_of(start + dr * o, dr), dr)]
    ws = take(1)
    push(wsend, wrecv, ws, mate)
    ours = pl.ds(pl.multiple_of(start + dr * p, dr), dr)
    wko[:, lanes(p)] = wtmp[0, ours]
    wqo[:, lanes(p)] = wtmp[1, ours]

    for k in reversed(yk):
        arrive(relo.at[ypeer(ny - k)], ms + k - 1)
        push(relo.at[ypeer(ny - k)], relq.at[ypeer(ny - k)], es + k, mate)
    arrive(wrecv, ws)
    wko[:, lanes(o)] = wrecv[0]
    wqo[:, lanes(o)] = wrecv[1]
    arrive(relq.at[y], es)
    for k in reversed(yk):
        arrive(relq.at[ypeer(ny - k)], es + k)
    for copy in sent:
        copy.wait_send()


def copy_kernel(dq, dk, dv, rel, relq, wk, wq, dqo, dko, dvo, relo, wqo, wko):
    p = lax.rem(lax.axis_index("seq"), 2)
    dqo[...] = dq[...]
    dko[...] = dk[...]
    dvo[...] = dv[...]
    relo[:, lanes(p)] = rel[...].reshape(relo.shape[0], T).astype(f32)
    relo[:, lanes(1 - p)] = relq[...].reshape(relo.shape[0], T).astype(f32)
    wqo[...] = wq[...]
    wko[...] = wk[...]


def body(ny, queries, keys, values, out_grad, rel_emb, w_query, w_key, doc_lengths, bucket_table):
    nc = lax.axis_size("seq") // 2
    nx = lax.axis_size("head")
    nz = nc // ny
    buckets, width = rel_emb.shape
    span = bucket_table.shape[0]
    rb = buckets // nc
    dr = width // nc // 2
    keys_in = TILES * T
    shape = jax.ShapeDtypeStruct
    tab = bucket_table.reshape(1, -1)
    lens = doc_lengths.reshape(1, -1)
    results = pl.pallas_call(
        functools.partial(whole_kernel, nz, ny, nx),
        out_shape=(
            shape((T, 2 * T), bf16),
            shape((T, 2 * T), bf16),
            shape((T, 2 * T), bf16),
            shape((ny, nz * rb, T), bf16),
            shape((ny, nz * rb, T), bf16),
            shape((dr, 2 * T), f32),
            shape((dr, 2 * T), f32),
        ),
        in_specs=[ANY] * 7 + [VM] * 2,
        out_specs=(VM,) * 7,
        scratch_shapes=[
            pltpu.VMEM((buckets, width), bf16),
            pltpu.VMEM((2, width, T), bf16),
            pltpu.VMEM((2 * T, T), bf16),
            pltpu.VMEM((2 * T, T), bf16),
            pltpu.VMEM((keys_in, T), bf16),
            pltpu.VMEM((keys_in, T), bf16),
            pltpu.VMEM((span, 2 * T), bf16),
            pltpu.VMEM((buckets, span), bf16),
            pltpu.VMEM((2, 2 * T, T), bf16),
            pltpu.VMEM((2, 2 * T, T), bf16),
            pltpu.VMEM((2, keys_in, T), bf16),
            pltpu.VMEM((2, span + 4 * T, T), bf16),
            pltpu.VMEM((T, 2 * T), bf16),
            pltpu.VMEM((T, keys_in), bf16),
            pltpu.VMEM((2, keys_in, 2 * T), f32),
            pltpu.VMEM((2, keys_in, 2 * T), f32),
            pltpu.VMEM((2, keys_in, 2 * T), bf16),
            pltpu.VMEM((2, keys_in, 2 * T), bf16),
            pltpu.VMEM((2, keys_in, 2 * T), bf16),
            pltpu.VMEM((2, keys_in, 3 * T), bf16),
            pltpu.VMEM((2, 2 * T, WIDE), bf16),
            pltpu.VMEM((2, 2 * T, span), bf16),
            pltpu.VMEM((keys_in, T), bf16),
            pltpu.VMEM((keys_in, T), bf16),
            pltpu.VMEM((2 * T, T), bf16),
            pltpu.VMEM((T, span), f32),
            pltpu.VMEM((T, span + 4 * T), f32),
            pltpu.VMEM((nc, 2 * rb, T), bf16),
            pltpu.VMEM((5, 2, 2, T, T), bf16),
            pltpu.VMEM((T, T), bf16),
            pltpu.VMEM((ny, nz, 2 * rb, T), bf16),
            pltpu.VMEM((nz, 2 * rb, T), bf16),
            pltpu.VMEM((nz, 2 * rb, T), bf16),
            pltpu.VMEM((2 * rb, T), bf16),
            pltpu.VMEM((nc, 2 * rb, T), bf16),
            pltpu.VMEM((2 * nx, rb, T), f32),
            pltpu.VMEM((2 * nx, rb, T), f32),
            pltpu.VMEM((nz, rb, T), f32),
            pltpu.VMEM((2, T, T), f32),
            pltpu.VMEM((2, dr, T), f32),
            pltpu.VMEM((2, dr, T), f32),
            pltpu.SemaphoreType.DMA((144,)),
            pltpu.SemaphoreType.DMA((144,)),
            pltpu.SemaphoreType.DMA((7,)),
        ],
        compiler_params=pltpu.CompilerParams(collective_id=0, has_side_effects=True),
        name="whole",
    )(queries, keys, values, out_grad, rel_emb, w_query, w_key, tab, lens)
    return tuple(
        pl.pallas_call(
            copy_kernel,
            out_shape=(
                shape((T, 2 * T), bf16),
                shape((T, 2 * T), bf16),
                shape((T, 2 * T), bf16),
                shape((buckets, 2 * T), f32),
                shape((dr, 2 * T), f32),
                shape((dr, 2 * T), f32),
            ),
            in_specs=[VM] * 7,
            out_specs=(VM,) * 6,
            name="results",
        )(*results)
    )


def solution(mesh, ny=NY):
    shard = P("seq", "head")
    return jax.shard_map(
        functools.partial(body, ny),
        mesh=mesh,
        in_specs=(shard,) * 4 + (P(), P(None, "head"), P(None, "head"), P(), P()),
        out_specs=(shard, shard, shard, P(None, "head"), shard, shard),
        check_vma=False,
    )
```

time: 99.5 us -> 69.7 us (0.70)
  Pallas kernels: 90.9 us -> 68.9 us
  local copies, waits for them, and re-layouts: 7.53 us -> 0 us
    pallas_call x3 -> x2, Pallas kernels: 90.9 us -> 68.9 us  [the longest x1 66.9 us: body(): pl.pallas_call(functools.partial(whole_kernel, nz, ny, nx), out_shape=(sh...]
    unnamed x14 -> x0, local copies, waits for them, and re-layouts: 6.18 us -> none
    rev x1 -> x0, local copies, waits for them, and re-layouts: 1.35 us -> none  [body(): rev = jnp.flip(bucket_table).reshape(1, -1)]
where the time goes in v2:
time: 69.7 us; the launch traced here: 69.5 us
  Pallas kernels  68.9 us (99%)
    pallas_call x1, Pallas kernels, body(): pl.pallas_call(functools.partial(whole_kernel, nz, ny, nx), out_shape=(sh...  66.9 us
    pallas_call x1, Pallas kernels, body(): pl.pallas_call(copy_kernel, out_shape=(shape((T, 2 * T), bf16), shape((T,...  1.97 us

profile of v2, /device:TPU:1, one launch (start us, length us, event | category | flops | bytes accessed | tf_op | source)
XLA Modules:
  0.0 69.5 jit_solution(10058188121187066117)
XLA Ops:
  0.6 66.9 %whole.1 = (bf16[128,256]{1,0:T(8,128)(2,1)}, bf16[128,256]{1,0:T(8,128)(2,1)}, bf16[128,256]{1,0:T(8,128)(2,1)}, bf16[4,128,128]{2,1,0:T(8,128)(2,1)}, bf16[4,1...) custom-call(bf16[128,256]{1,0:T(8,128)(2,1)} %q_ref.1, bf16[128,256]{1,0:T(8,128)(2,1)} %k_ref.1, ...), custom_call_target="tpu_custom_call" | custom-call | tf_op jit(solution)/shard_map/whole/pallas_call | solution.py:465
  67.6 2.0 %results.1 = (bf16[128,256]{1,0:T(8,128)(2,1)}, bf16[128,256]{1,0:T(8,128)(2,1)}, bf16[128,256]{1,0:T(8,128)(2,1)}, f32[512,256]{1,0:T(8,128)}, f32[8,256]{1,0:T(8,128)}, /*index=5*/f32[8,256]{1,0:T(8,128)}) custom-call(bf16[128,256]{1,0:T(8,128)(2,1)} %get-tuple-element.13.dq, bf16[128,256]{1,0:T(8,128)(2,1)} %get-tuple-element.14.dk, ...), custom_call_target="tpu_custom_call" | custom-call | tf_op jit(solution)/shard_map/results/pallas_call | solution.py:528

commit v3 on v2

--- a/solution.py
+++ b/solution.py
@@ -71,7 +71,7 @@
     q_ref, k_ref, v_ref, g_ref, rel_ref, wq_ref, wk_ref, tab_ref, len_ref,
     dqo, dko, dvo, relo, relq, wko, wqo,
     rel_v, wv, qw, gw, kw, vw, pb, oht, q2, g2, k2, pqr, qrt, krt,
-    sc, dp, prb, dsb, dsr, skb, dsa, ska, dkb, dvb, dqb, gt, ht,
+    sc, dp, dsb, dsr, skb, dsa, ska, dkb, dvb, dqb, gt, ht,
     bp, rkv, rq, yrecv, zsend, zrecv, own, ag, xpart, xrecv, relz,
     wtmp, wsend, wrecv, send, recv, local,
 ):
@@ -135,6 +135,40 @@
     load(q_ref.at[:, lanes(p)], qw.at[rows(T * p)])
     load(g_ref.at[:, lanes(p)], gw.at[rows(T * p)])
 
+    pl.semaphore_wait(
+        pltpu.get_barrier_semaphore(), len(zk) + len(yk) + 8 + len(mk) + 1
+    )
+
+    sent = []
+    slots = [0]
+
+    def push(src, dst, slot, seq, head=None):
+        copy = remote(src, dst, send.at[len(sent)], recv.at[slot], seq, head)
+        copy.start()
+        sent.append(copy)
+
+    def take(count):
+        base = slots[0]
+        slots[0] += count
+        return base
+
+    def arrive(dst, slot):
+        remote(dst, dst, send.at[0], recv.at[slot], s).wait_recv()
+
+    near = take(4)
+    hs = take(20)
+    row = rows(T * p)
+    push(q_ref.at[:, lanes(o)], qw.at[row], near, mate)
+    push(g_ref.at[:, lanes(o)], gw.at[row], near + 1, mate)
+    row = rows(2 * HALO * T + T * p)
+    push(k_ref.at[:, lanes(o)], kw.at[row], near + 2, mate)
+    push(v_ref.at[:, lanes(o)], vw.at[row], near + 3, mate)
+    for d in hops:
+        for pp in range(2):
+            row = rows(2 * T * (HALO - d) + T * p)
+            base = hs + ((d + HALO) * 2 + p) * 2
+            push(k_ref.at[:, pl.ds(pp * T, T)], kw.at[row], base, 2 * chip(d) + pp)
+            push(v_ref.at[:, pl.ds(pp * T, T)], vw.at[row], base + 1, 2 * chip(d) + pp)
     ri = lax.broadcasted_iota(jnp.int32, (T, T), 0)
     ci = lax.broadcasted_iota(jnp.int32, (T, T), 1)
     flip = indicator(ri + ci == T - 1)
@@ -180,40 +214,6 @@
         pqr[h, 2 * T + span :] = jnp.zeros((2 * T, T), bf16)
     ht[...] = jnp.zeros_like(ht)
 
-    pl.semaphore_wait(
-        pltpu.get_barrier_semaphore(), len(zk) + len(yk) + 8 + len(mk) + 1
-    )
-
-    sent = []
-    slots = [0]
-
-    def push(src, dst, slot, seq, head=None):
-        copy = remote(src, dst, send.at[len(sent)], recv.at[slot], seq, head)
-        copy.start()
-        sent.append(copy)
-
-    def take(count):
-        base = slots[0]
-        slots[0] += count
-        return base
-
-    def arrive(dst, slot):
-        remote(dst, dst, send.at[0], recv.at[slot], s).wait_recv()
-
-    near = take(4)
-    hs = take(20)
-    row = rows(T * p)
-    push(q_ref.at[:, lanes(o)], qw.at[row], near, mate)
-    push(g_ref.at[:, lanes(o)], gw.at[row], near + 1, mate)
-    row = rows(2 * HALO * T + T * p)
-    push(k_ref.at[:, lanes(o)], kw.at[row], near + 2, mate)
-    push(v_ref.at[:, lanes(o)], vw.at[row], near + 3, mate)
-    for d in hops:
-        for pp in range(2):
-            row = rows(2 * T * (HALO - d) + T * p)
-            base = hs + ((d + HALO) * 2 + p) * 2
-            push(k_ref.at[:, pl.ds(pp * T, T)], kw.at[row], base, 2 * chip(d) + pp)
-            push(v_ref.at[:, pl.ds(pp * T, T)], vw.at[row], base + 1, 2 * chip(d) + pp)
     for copy in loads[3:]:
         copy.wait()
     arrive(qw.at[rows(T * o)], near)
@@ -269,6 +269,7 @@
         score(2 * (HALO + d))
         score(2 * (HALO + d) + 1)
 
+    inv, row_dot = [], []
     for h in range(2):
         high_score = jnp.max(top[h], axis=0, keepdims=True)
         total = jnp.zeros((8, 2 * T), f32)
@@ -278,13 +279,33 @@
             sc[h, tile(j)] = x
             total = total + fold(x, jnp.sum)
             along = along + fold(x * dp[h, tile(j)], jnp.sum)
-        inv = 1.0 / jnp.sum(total, axis=0, keepdims=True)
-        row_dot = jnp.sum(along, axis=0, keepdims=True) * inv
+        inv.append(1.0 / jnp.sum(total, axis=0, keepdims=True))
+        row_dot.append(jnp.sum(along, axis=0, keepdims=True) * inv[h])
+
+    far_first = [j for d in (-2, 2, -1, 1, 0) for j in (2 * (d + HALO), 2 * (d + HALO) + 1)]
+    for j in far_first:
+        dv = jnp.zeros((T, T), f32)
+        for h in range(2):
+            prob = (sc[h, tile(j)] * inv[h]).astype(bf16)
+            dv = dv + dot(prob, g2[h])
+        dvb[tile(j)] = dv.astype(bf16)
+    rs = take(20)
+
+    def give_back(grad, i):
+        for d in reversed(hops):
+            for pp in range(2):
+                push(grad.at[tile(2 * (d + HALO) + pp)], rkv.at[d + HALO, p, i],
+                     rs + ((d + HALO) * 2 + p) * 2 + i, 2 * chip(d) + pp)
+        push(grad.at[rows(2 * HALO * T + T * o)], rkv.at[HALO, p, i],
+             rs + (HALO * 2 + p) * 2 + i, mate)
+
+    give_back(dvb, 1)
+
+    for h in range(2):
         half = slice(h * HD, (h + 1) * HD)
         for j in range(TILES):
-            prob = sc[h, tile(j)] * inv
-            ds = (prob * (dp[h, tile(j)] - row_dot)).astype(bf16)
-            prb[h, tile(j)] = prob.astype(bf16)
+            prob = sc[h, tile(j)] * inv[h]
+            ds = (prob * (dp[h, tile(j)] - row_dot[h])).astype(bf16)
             dsb[h, tile(j)] = ds
             back = dot(flip, ds)
             dsr[h, tile(j)] = back.astype(bf16)
@@ -310,9 +331,7 @@
     for k in yk:
         push(bp.at[pl.ds(nz * ypeer(k), nz)], yrecv.at[k - 1], ys + k - 1, at(z, ypeer(k)))
 
-    for j in (0, 1, 8, 9, 2, 3, 6, 7, 4, 5):
-        dv = dot(prb[0, tile(j)], g2[0]) + dot(prb[1, tile(j)], g2[1])
-        dvb[tile(j)] = dv.astype(bf16)
+    for j in far_first:
         dk = dot(dsr[0, tile(j)], q2[0]) + dot(dsr[1, tile(j)], q2[1])
         dk = dk + dot(skb[0, tile(j)], pqr[0, band(j)]) + dot(skb[1, tile(j)], pqr[1, band(j)])
         dkb[tile(j)] = dot(flip, (SCALE * dk).astype(bf16)).astype(bf16)
@@ -334,19 +353,9 @@
     for k in zk:
         push(zsend.at[zpeer(k)], zrecv.at[k - 1], zs + k - 1, at(zpeer(k), y))
 
-    rs = take(20)
     qs = take(1)
-    for d in hops:
-        for pp in range(2):
-            row = tile(2 * (d + HALO) + pp)
-            slot = rs + ((d + HALO) * 2 + p) * 2
-            push(dkb.at[row], rkv.at[d + HALO, p, 0], slot, 2 * chip(d) + pp)
-            push(dvb.at[row], rkv.at[d + HALO, p, 1], slot + 1, 2 * chip(d) + pp)
-    row = rows(2 * HALO * T + T * o)
-    slot = rs + (HALO * 2 + p) * 2
-    push(dkb.at[row], rkv.at[HALO, p, 0], slot, mate)
-    push(dvb.at[row], rkv.at[HALO, p, 1], slot + 1, mate)
     push(dqb.at[rows(T * o)], rq, qs, mate)
+    give_back(dkb, 0)
 
     part = zsend[z].astype(f32)
     for k in reversed(zk):
@@ -383,6 +392,29 @@
     mine = pl.ds(nz * y, nz)
     for k in yk:
         push(ag.at[mine], ag.at[mine], us + k - 1, at(z, ypeer(k)))
+
+    for k in reversed(yk):
+        arrive(ag.at[pl.ds(nz * ypeer(ny - k), nz)], us + k - 1)
+    every = ag[...].astype(f32)
+    for i in range(2):
+        grad = every[:, i * rb : (i + 1) * rb].reshape(buckets, T).astype(bf16)
+        wtmp[i] = dot(rel_v[:, lanes(c * dr2 // T)], grad, 0, 0)
+    start = lax.rem(c * dr2, T)
+    wsend[...] = wtmp[:, pl.ds(pl.multiple_of(start + dr * o, dr), dr)]
+    ws = take(1)
+    push(wsend, wrecv, ws, mate)
+    ours = pl.ds(pl.multiple_of(start + dr * p, dr), dr)
+    wko[:, lanes(p)] = wtmp[0, ours]
+    wqo[:, lanes(p)] = wtmp[1, ours]
+
+    for k in reversed(zk):
+        arrive(relz.at[zpeer(nz - k)], ls + k - 1)
+    relo[y] = relz[...].reshape(nz * rb, T).astype(bf16)
+    ms = take(ny)
+    es = take(ny)
+    for k in yk:
+        push(relo.at[y], relo.at[y], ms + k - 1, at(z, ypeer(k)))
+    push(relo.at[y], relq.at[y], es, mate)
 
     dqo[:, lanes(p)] = dqb[rows(T * p)]
     arrive(rq, qs)
@@ -402,29 +434,6 @@
             for d in range(1, 2 * HALO + 1):
                 x = x + rkv[d, pp, i].astype(f32)
             out[:, tile(pp)] = x.astype(bf16)
-
-    for k in reversed(zk):
-        arrive(relz.at[zpeer(nz - k)], ls + k - 1)
-    relo[y] = relz[...].reshape(nz * rb, T).astype(bf16)
-    ms = take(ny)
-    es = take(ny)
-    for k in yk:
-        push(relo.at[y], relo.at[y], ms + k - 1, at(z, ypeer(k)))
-    push(relo.at[y], relq.at[y], es, mate)
-
-    for k in reversed(yk):
-        arrive(ag.at[pl.ds(nz * ypeer(ny - k), nz)], us + k - 1)
-    every = ag[...].astype(f32)
-    for i in range(2):
-        grad = every[:, i * rb : (i + 1) * rb].reshape(buckets, T).astype(bf16)
-        wtmp[i] = dot(rel_v[:, lanes(c * dr2 // T)], grad, 0, 0)
-    start = lax.rem(c * dr2, T)
-    wsend[...] = wtmp[:, pl.ds(pl.multiple_of(start + dr * o, dr), dr)]
-    ws = take(1)
-    push(wsend, wrecv, ws, mate)
-    ours = pl.ds(pl.multiple_of(start + dr * p, dr), dr)
-    wko[:, lanes(p)] = wtmp[0, ours]
-    wqo[:, lanes(p)] = wtmp[1, ours]
 
     for k in reversed(yk):
         arrive(relo.at[ypeer(ny - k)], ms + k - 1)
@@ -492,7 +501,6 @@
             pltpu.VMEM((T, keys_in), bf16),
             pltpu.VMEM((2, keys_in, 2 * T), f32),
             pltpu.VMEM((2, keys_in, 2 * T), f32),
-            pltpu.VMEM((2, keys_in, 2 * T), bf16),
             pltpu.VMEM((2, keys_in, 2 * T), bf16),
             pltpu.VMEM((2, keys_in, 2 * T), bf16),
             pltpu.VMEM((2, keys_in, 3 * T), bf16),

time: 69.7 us -> 70.9 us (1.017)
  Pallas kernels: 68.9 us -> 70.1 us
    pallas_call x1, Pallas kernels: 66.9 us -> 68.1 us  [body(): pl.pallas_call(functools.partial(whole_kernel, nz, ny, nx), out_shape=(sh...]
where the time goes in v3:
time: 70.9 us; the launch traced here: 70.7 us
  Pallas kernels  70.1 us (99%)
    pallas_call x1, Pallas kernels, body(): pl.pallas_call(functools.partial(whole_kernel, nz, ny, nx), out_shape=(sh...  68.1 us
    pallas_call x1, Pallas kernels, body(): pl.pallas_call(copy_kernel, out_shape=(shape((T, 2 * T), bf16), shape((T,...  1.97 us

profile of v3, /device:TPU:1, one launch (start us, length us, event | category | flops | bytes accessed | tf_op | source)
XLA Modules:
  0.0 70.7 jit_solution(4322558742526276596)
XLA Ops:
  0.6 68.1 %whole.1 = (bf16[128,256]{1,0:T(8,128)(2,1)}, bf16[128,256]{1,0:T(8,128)(2,1)}, bf16[128,256]{1,0:T(8,128)(2,1)}, bf16[4,128,128]{2,1,0:T(8,128)(2,1)}, bf16[4,1...) custom-call(bf16[128,256]{1,0:T(8,128)(2,1)} %q_ref.1, bf16[128,256]{1,0:T(8,128)(2,1)} %k_ref.1, ...), custom_call_target="tpu_custom_call" | custom-call | tf_op jit(solution)/shard_map/whole/pallas_call | solution.py:474
  68.7 2.0 %results.1 = (bf16[128,256]{1,0:T(8,128)(2,1)}, bf16[128,256]{1,0:T(8,128)(2,1)}, bf16[128,256]{1,0:T(8,128)(2,1)}, f32[512,256]{1,0:T(8,128)}, f32[8,256]{1,0:T(8,128)}, /*index=5*/f32[8,256]{1,0:T(8,128)}) custom-call(bf16[128,256]{1,0:T(8,128)(2,1)} %get-tuple-element.13.dq, bf16[128,256]{1,0:T(8,128)(2,1)} %get-tuple-element.14.dk, ...), custom_call_target="tpu_custom_call" | custom-call | tf_op jit(solution)/shard_map/results/pallas_call | solution.py:536

commit v4 on v3

--- a/solution.py
+++ b/solution.py
@@ -71,9 +71,9 @@
     q_ref, k_ref, v_ref, g_ref, rel_ref, wq_ref, wk_ref, tab_ref, len_ref,
     dqo, dko, dvo, relo, relq, wko, wqo,
     rel_v, wv, qw, gw, kw, vw, pb, oht, q2, g2, k2, pqr, qrt, krt,
-    sc, dp, dsb, dsr, skb, dsa, ska, dkb, dvb, dqb, gt, ht,
+    sc, dp, prb, dsb, dsr, skb, dsa, ska, dkb, dvb, dqb, gt, ht,
     bp, rkv, rq, yrecv, zsend, zrecv, own, ag, xpart, xrecv, relz,
-    wtmp, wsend, wrecv, send, recv, local,
+    wtmp, wsend, wrecv, send, recv, local, known,
 ):
     nc = nz * ny
     s = lax.axis_index("seq")
@@ -109,7 +109,7 @@
     zk = sorted(range(1, nz), key=lambda k: -min(k, nz - k))
     mk = range(1, 2 * nx)
 
-    for k in zk:
+    for k in (1, nz - 1):
         greet(at(zpeer(k), y))
     for k in yk:
         greet(at(z, ypeer(k)))
@@ -136,7 +136,7 @@
     load(g_ref.at[:, lanes(p)], gw.at[rows(T * p)])
 
     pl.semaphore_wait(
-        pltpu.get_barrier_semaphore(), len(zk) + len(yk) + 8 + len(mk) + 1
+        pltpu.get_barrier_semaphore(), 2 + len(yk) + 8 + len(mk) + 1
     )
 
     sent = []
@@ -155,20 +155,46 @@
     def arrive(dst, slot):
         remote(dst, dst, send.at[0], recv.at[slot], s).wait_recv()
 
+    step = [1 << i for i in range(nz.bit_length()) if (1 << i) < nz // 2]
+
+    def tell(i):
+        if i < len(step):
+            for k in (step[i], nz - step[i]):
+                pl.semaphore_signal(known.at[i], inc=1, device_id={"seq": at(zpeer(k), y)},
+                                    device_id_type=pl.DeviceIdType.MESH)
+
+    def hear(i):
+        if i < len(step):
+            pl.semaphore_wait(known.at[i], 2)
+
     near = take(4)
-    hs = take(20)
+    hs = take(8)
+    fs = take(4)
     row = rows(T * p)
     push(q_ref.at[:, lanes(o)], qw.at[row], near, mate)
     push(g_ref.at[:, lanes(o)], gw.at[row], near + 1, mate)
     row = rows(2 * HALO * T + T * p)
     push(k_ref.at[:, lanes(o)], kw.at[row], near + 2, mate)
     push(v_ref.at[:, lanes(o)], vw.at[row], near + 3, mate)
-    for d in hops:
-        for pp in range(2):
-            row = rows(2 * T * (HALO - d) + T * p)
-            base = hs + ((d + HALO) * 2 + p) * 2
-            push(k_ref.at[:, pl.ds(pp * T, T)], kw.at[row], base, 2 * chip(d) + pp)
-            push(v_ref.at[:, pl.ds(pp * T, T)], vw.at[row], base + 1, 2 * chip(d) + pp)
+    for i, src, dst in ((0, k_ref, kw), (1, v_ref, vw)):
+        for d in (-1, 1):
+            for pp in range(2):
+                push(src.at[:, pl.ds(pp * T, T)], dst.at[rows(2 * T * (HALO - d) + T * p)],
+                     hs + (d + 1) * 2 + p * 2 + i, 2 * chip(d) + pp)
+    tell(0)
+
+    def pass_on(i, ref):
+        for d in (-1, 1):
+            for pp in range(2):
+                arrive(ref.at[tile(2 * (HALO + d) + pp)], hs + (1 - d) * 2 + pp * 2 + i)
+            near_rows = pl.ds(2 * T * (HALO + d), 2 * T)
+            far_rows = pl.ds(2 * T * (HALO + 2 * d), 2 * T)
+            push(ref.at[near_rows], ref.at[far_rows], fs + d + 1 + i, 2 * chip(-d) + p)
+
+    def passed(i, ref):
+        for d in (-1, 1):
+            arrive(ref.at[pl.ds(2 * T * (HALO + 2 * d), 2 * T)], fs + d + 1 + i)
+
     ri = lax.broadcasted_iota(jnp.int32, (T, T), 0)
     ci = lax.broadcasted_iota(jnp.int32, (T, T), 1)
     flip = indicator(ri + ci == T - 1)
@@ -206,6 +232,7 @@
     for copy in loads[:3]:
         copy.wait()
     pos_key = dot(rel_v[...], wv[0]).astype(bf16)
+    pass_on(0, kw)
     pos_query = dot(rel_v[...], wv[1]).astype(bf16)
     pb[...] = dot(onehot, jnp.concatenate([pos_key, pos_query], 1)).astype(bf16)
     for h in range(2):
@@ -214,8 +241,11 @@
         pqr[h, 2 * T + span :] = jnp.zeros((2 * T, T), bf16)
     ht[...] = jnp.zeros_like(ht)
 
+    hear(0)
+    tell(1)
     for copy in loads[3:]:
         copy.wait()
+    pass_on(1, vw)
     arrive(qw.at[rows(T * o)], near)
     arrive(gw.at[rows(T * o)], near + 1)
 
@@ -256,18 +286,24 @@
             x = jnp.where(keep, x, -1e30)
             sc[h, tile(j)] = x
             top[h] = jnp.maximum(top[h], fold(x, jnp.max))
+
+    def through_values(j):
+        for h in range(2):
             dp[h, tile(j)] = dot(vw[tile(j)], g2[h], 1, 1)
 
-    score(4)
-    score(5)
-    for d in (-1, 1, -2, 2):
-        for pp in range(2):
-            j = 2 * (HALO - (-d)) + pp
-            base = hs + ((-d + HALO) * 2 + pp) * 2
-            arrive(kw.at[tile(j)], base)
-            arrive(vw.at[tile(j)], base + 1)
-        score(2 * (HALO + d))
-        score(2 * (HALO + d) + 1)
+    inner, outer = (4, 5, 2, 3, 6, 7), (0, 1, 8, 9)
+    for j in inner:
+        score(j)
+    hear(1)
+    tell(2)
+    for j in inner:
+        through_values(j)
+    passed(0, kw)
+    for j in outer:
+        score(j)
+    passed(1, vw)
+    for j in outer:
+        through_values(j)
 
     inv, row_dot = [], []
     for h in range(2):
@@ -282,30 +318,12 @@
         inv.append(1.0 / jnp.sum(total, axis=0, keepdims=True))
         row_dot.append(jnp.sum(along, axis=0, keepdims=True) * inv[h])
 
-    far_first = [j for d in (-2, 2, -1, 1, 0) for j in (2 * (d + HALO), 2 * (d + HALO) + 1)]
-    for j in far_first:
-        dv = jnp.zeros((T, T), f32)
-        for h in range(2):
-            prob = (sc[h, tile(j)] * inv[h]).astype(bf16)
-            dv = dv + dot(prob, g2[h])
-        dvb[tile(j)] = dv.astype(bf16)
-    rs = take(20)
-
-    def give_back(grad, i):
-        for d in reversed(hops):
-            for pp in range(2):
-                push(grad.at[tile(2 * (d + HALO) + pp)], rkv.at[d + HALO, p, i],
-                     rs + ((d + HALO) * 2 + p) * 2 + i, 2 * chip(d) + pp)
-        push(grad.at[rows(2 * HALO * T + T * o)], rkv.at[HALO, p, i],
-             rs + (HALO * 2 + p) * 2 + i, mate)
-
-    give_back(dvb, 1)
-
     for h in range(2):
         half = slice(h * HD, (h + 1) * HD)
         for j in range(TILES):
             prob = sc[h, tile(j)] * inv[h]
             ds = (prob * (dp[h, tile(j)] - row_dot[h])).astype(bf16)
+            prb[h, tile(j)] = prob.astype(bf16)
             dsb[h, tile(j)] = ds
             back = dot(flip, ds)
             dsr[h, tile(j)] = back.astype(bf16)
@@ -331,7 +349,10 @@
     for k in yk:
         push(bp.at[pl.ds(nz * ypeer(k), nz)], yrecv.at[k - 1], ys + k - 1, at(z, ypeer(k)))
 
+    far_first = [j for d in (-2, 2, -1, 1, 0) for j in (2 * (d + HALO), 2 * (d + HALO) + 1)]
     for j in far_first:
+        dv = dot(prb[0, tile(j)], g2[0]) + dot(prb[1, tile(j)], g2[1])
+        dvb[tile(j)] = dv.astype(bf16)
         dk = dot(dsr[0, tile(j)], q2[0]) + dot(dsr[1, tile(j)], q2[1])
         dk = dk + dot(skb[0, tile(j)], pqr[0, band(j)]) + dot(skb[1, tile(j)], pqr[1, band(j)])
         dkb[tile(j)] = dot(flip, (SCALE * dk).astype(bf16)).astype(bf16)
@@ -349,13 +370,25 @@
         part = part + yrecv[k - 1].astype(f32)
     zsend[...] = part.astype(bf16)
 
+    hear(2)
     zs = take(nz)
     for k in zk:
         push(zsend.at[zpeer(k)], zrecv.at[k - 1], zs + k - 1, at(zpeer(k), y))
 
+    rs = take(20)
+
+    def give_back(grad, i):
+        for d in reversed(hops):
+            for pp in range(2):
+                push(grad.at[tile(2 * (d + HALO) + pp)], rkv.at[d + HALO, p, i],
+                     rs + ((d + HALO) * 2 + p) * 2 + i, 2 * chip(d) + pp)
+        push(grad.at[rows(2 * HALO * T + T * o)], rkv.at[HALO, p, i],
+             rs + (HALO * 2 + p) * 2 + i, mate)
+
     qs = take(1)
     push(dqb.at[rows(T * o)], rq, qs, mate)
     give_back(dkb, 0)
+    give_back(dvb, 1)
 
     part = zsend[z].astype(f32)
     for k in reversed(zk):
@@ -503,6 +536,7 @@
             pltpu.VMEM((2, keys_in, 2 * T), f32),
             pltpu.VMEM((2, keys_in, 2 * T), bf16),
             pltpu.VMEM((2, keys_in, 2 * T), bf16),
+            pltpu.VMEM((2, keys_in, 2 * T), bf16),
             pltpu.VMEM((2, keys_in, 3 * T), bf16),
             pltpu.VMEM((2, 2 * T, WIDE), bf16),
             pltpu.VMEM((2, 2 * T, span), bf16),
@@ -528,6 +562,7 @@
             pltpu.SemaphoreType.DMA((144,)),
             pltpu.SemaphoreType.DMA((144,)),
             pltpu.SemaphoreType.DMA((7,)),
+            pltpu.SemaphoreType.REGULAR((3,)),
         ],
         compiler_params=pltpu.CompilerParams(collective_id=0, has_side_effects=True),
         name="whole",

time: 70.9 us -> 66.5 us (0.938)
  Pallas kernels: 70.1 us -> 65.6 us
    pallas_call x1, Pallas kernels: 68.1 us -> 63.7 us  [body(): pl.pallas_call(functools.partial(whole_kernel, nz, ny, nx), out_shape=(sh...]
where the time goes in v4:
time: 66.5 us; the launch traced here: 66.3 us
  Pallas kernels  65.6 us (99%)
    pallas_call x1, Pallas kernels, body(): pl.pallas_call(functools.partial(whole_kernel, nz, ny, nx), out_shape=(sh...  63.7 us
    pallas_call x1, Pallas kernels, body(): pl.pallas_call(copy_kernel, out_shape=(shape((T, 2 * T), bf16), shape((T,...  1.97 us

profile of v4, /device:TPU:1, one launch (start us, length us, event | category | flops | bytes accessed | tf_op | source)
XLA Modules:
  0.0 66.3 jit_solution(14412699061400975318)
XLA Ops:
  0.6 63.7 %whole.1 = (bf16[128,256]{1,0:T(8,128)(2,1)}, bf16[128,256]{1,0:T(8,128)(2,1)}, bf16[128,256]{1,0:T(8,128)(2,1)}, bf16[4,128,128]{2,1,0:T(8,128)(2,1)}, bf16[4,1...) custom-call(bf16[128,256]{1,0:T(8,128)(2,1)} %q_ref.1, bf16[128,256]{1,0:T(8,128)(2,1)} %k_ref.1, ...), custom_call_target="tpu_custom_call" | custom-call | tf_op jit(solution)/shard_map/whole/pallas_call | solution.py:507
  64.3 2.0 %results.1 = (bf16[128,256]{1,0:T(8,128)(2,1)}, bf16[128,256]{1,0:T(8,128)(2,1)}, bf16[128,256]{1,0:T(8,128)(2,1)}, f32[512,256]{1,0:T(8,128)}, f32[8,256]{1,0:T(8,128)}, /*index=5*/f32[8,256]{1,0:T(8,128)}) custom-call(bf16[128,256]{1,0:T(8,128)(2,1)} %get-tuple-element.13.dq, bf16[128,256]{1,0:T(8,128)(2,1)} %get-tuple-element.14.dk, ...), custom_call_target="tpu_custom_call" | custom-call | tf_op jit(solution)/shard_map/results/pallas_call | solution.py:571

commit v5 on v4

--- a/solution.py
+++ b/solution.py
@@ -73,7 +73,7 @@
     rel_v, wv, qw, gw, kw, vw, pb, oht, q2, g2, k2, pqr, qrt, krt,
     sc, dp, prb, dsb, dsr, skb, dsa, ska, dkb, dvb, dqb, gt, ht,
     bp, rkv, rq, yrecv, zsend, zrecv, own, ag, xpart, xrecv, relz,
-    wtmp, wsend, wrecv, send, recv, local, known,
+    wtmp, wy, wsum, wrecv, send, recv, local, known,
 ):
     nc = nz * ny
     s = lax.axis_index("seq")
@@ -105,6 +105,9 @@
     def at(zz, yy):
         return 2 * (zz * ny + yy) + p
 
+    def plane(yy):
+        return pl.ds(pl.multiple_of(nz * rb * yy, nz * rb), nz * rb)
+
     yk = sorted(range(1, ny), key=lambda k: -min(k, ny - k))
     zk = sorted(range(1, nz), key=lambda k: -min(k, nz - k))
     mk = range(1, 2 * nx)
@@ -113,7 +116,7 @@
         greet(at(zpeer(k), y))
     for k in yk:
         greet(at(z, ypeer(k)))
-    for d in hops:
+    for d in (-1, 1):
         for pp in range(2):
             greet(2 * chip(d) + pp)
     for k in mk:
@@ -136,7 +139,7 @@
     load(g_ref.at[:, lanes(p)], gw.at[rows(T * p)])
 
     pl.semaphore_wait(
-        pltpu.get_barrier_semaphore(), 2 + len(yk) + 8 + len(mk) + 1
+        pltpu.get_barrier_semaphore(), 2 + len(yk) + 4 + len(mk) + 1
     )
 
     sent = []
@@ -330,6 +333,18 @@
             skew = skewed(jnp.concatenate([back, jnp.zeros((T, T), f32)], 1), 0).astype(bf16)
             skb[h, tile(j)] = skew
             ht[half, band(j)] += dot(krt[half, tile(j)], skew)
+
+    ys = take(2 * ny)
+
+    def scatter(i, offsets):
+        bp[i] = (SCALE * dot(oht[...], offsets.astype(bf16), 1, 1)).astype(bf16)
+        for k in yk:
+            push(bp.at[i, plane(ypeer(k))], yrecv.at[i, k - 1],
+                 ys + i * ny + k - 1, at(z, ypeer(k)))
+
+    scatter(1, ht[:, 2 * T : 2 * T + span])
+    for h in range(2):
+        half = slice(h * HD, (h + 1) * HD)
         for r in range(2):
             back = dot(flip, dsb[h, r * T : r * T + WIDE, tile(r)], 1, 1)
             dsa[h, tile(r)] = back.astype(bf16)
@@ -340,22 +355,12 @@
                 gt[half] = part
             else:
                 gt[half] += part
-
-    bk = SCALE * dot(oht[...], gt[...].astype(bf16), 1, 1)
-    bq = SCALE * dot(oht[...], ht[:, 2 * T : 2 * T + span].astype(bf16), 1, 1)
-    bp[...] = jnp.concatenate([bk.reshape(nc, rb, T), bq.reshape(nc, rb, T)], 1).astype(bf16)
-
-    ys = take(ny)
-    for k in yk:
-        push(bp.at[pl.ds(nz * ypeer(k), nz)], yrecv.at[k - 1], ys + k - 1, at(z, ypeer(k)))
+    scatter(0, gt[...])
 
     far_first = [j for d in (-2, 2, -1, 1, 0) for j in (2 * (d + HALO), 2 * (d + HALO) + 1)]
     for j in far_first:
         dv = dot(prb[0, tile(j)], g2[0]) + dot(prb[1, tile(j)], g2[1])
         dvb[tile(j)] = dv.astype(bf16)
-        dk = dot(dsr[0, tile(j)], q2[0]) + dot(dsr[1, tile(j)], q2[1])
-        dk = dk + dot(skb[0, tile(j)], pqr[0, band(j)]) + dot(skb[1, tile(j)], pqr[1, band(j)])
-        dkb[tile(j)] = dot(flip, (SCALE * dk).astype(bf16)).astype(bf16)
     for r in range(2):
         reach = slice(r * T, r * T + WIDE)
         dq = dot(dsa[0, tile(r)], k2[0, reach]) + dot(dsa[1, tile(r)], k2[1, reach])
@@ -363,18 +368,25 @@
             dq = dq + head_only(dot(ska[h, tile(r)], pb[:, :T]), h)
         dqb[tile(r)] = dot(flip, (SCALE * dq).astype(bf16)).astype(bf16)
 
-    part = bp[pl.ds(nz * y, nz)].astype(f32)
-    for k in yk:
-        arrive(yrecv.at[k - 1], ys + k - 1)
-    for k in yk:
-        part = part + yrecv[k - 1].astype(f32)
-    zsend[...] = part.astype(bf16)
+    parts = []
+    for i in range(2):
+        part = bp[i, plane(y)].astype(f32)
+        for k in yk:
+            arrive(yrecv.at[i, k - 1], ys + i * ny + k - 1)
+        for k in yk:
+            part = part + yrecv[i, k - 1].astype(f32)
+        parts.append(part.reshape(nz, rb, T))
+    zsend[...] = jnp.concatenate(parts, 1).astype(bf16)
 
     hear(2)
     zs = take(nz)
     for k in zk:
         push(zsend.at[zpeer(k)], zrecv.at[k - 1], zs + k - 1, at(zpeer(k), y))
 
+    for j in far_first:
+        dk = dot(dsr[0, tile(j)], q2[0]) + dot(dsr[1, tile(j)], q2[1])
+        dk = dk + dot(skb[0, tile(j)], pqr[0, band(j)]) + dot(skb[1, tile(j)], pqr[1, band(j)])
+        dkb[tile(j)] = dot(flip, (SCALE * dk).astype(bf16)).astype(bf16)
     rs = take(20)
 
     def give_back(grad, i):
@@ -387,8 +399,8 @@
 
     qs = take(1)
     push(dqb.at[rows(T * o)], rq, qs, mate)
+    give_back(dvb, 1)
     give_back(dkb, 0)
-    give_back(dvb, 1)
 
     part = zsend[z].astype(f32)
     for k in reversed(zk):
@@ -396,11 +408,7 @@
         part = part + zrecv[k - 1].astype(f32)
     low = part.astype(bf16)
     own[...] = low
-    ag[nz * y + z] = low
-
-    gs = take(nz)
-    for k in zk:
-        push(own, ag.at[nz * y + z], gs + k - 1, at(zpeer(k), y))
+    ag[z] = low
 
     both = low.astype(f32)
     rel_part = dot(both[:rb].astype(bf16), wv[0], 1, 1) + dot(both[rb:].astype(bf16), wv[1], 1, 1)
@@ -410,48 +418,57 @@
     for k in mk:
         push(xpart.at[mpeer(k)], xrecv.at[k - 1], xs + k - 1,
              2 * c + lax.rem(mpeer(k), 2), mpeer(k) // 2)
+
+    gs = take(nz)
+    for k in zk:
+        push(own, ag.at[z], gs + k - 1, at(zpeer(k), y))
     total = xpart[m]
     for k in mk:
         arrive(xrecv.at[k - 1], xs + k - 1)
         total = total + xrecv[k - 1]
-    relz[z] = total
+    relz[z] = total.astype(bf16)
     ls = take(nz)
     for k in zk:
         push(relz.at[z], relz.at[z], ls + k - 1, at(zpeer(k), y))
 
     for k in reversed(zk):
-        arrive(ag.at[nz * y + zpeer(nz - k)], gs + k - 1)
-    us = take(ny)
-    mine = pl.ds(nz * y, nz)
-    for k in yk:
-        push(ag.at[mine], ag.at[mine], us + k - 1, at(z, ypeer(k)))
-
-    for k in reversed(yk):
-        arrive(ag.at[pl.ds(nz * ypeer(ny - k), nz)], us + k - 1)
+        arrive(ag.at[zpeer(nz - k)], gs + k - 1)
     every = ag[...].astype(f32)
     for i in range(2):
-        grad = every[:, i * rb : (i + 1) * rb].reshape(buckets, T).astype(bf16)
-        wtmp[i] = dot(rel_v[:, lanes(c * dr2 // T)], grad, 0, 0)
-    start = lax.rem(c * dr2, T)
-    wsend[...] = wtmp[:, pl.ds(pl.multiple_of(start + dr * o, dr), dr)]
+        grad = every[:, i * rb : (i + 1) * rb].reshape(nz * rb, T).astype(bf16)
+        block = rel_v[plane(y), lanes(z * ny * dr2 // T)]
+        wtmp[i] = dot(block, grad, 0, 0)
+    start = lax.rem(z * ny * dr2, T)
+
+    def of(yy):
+        return pl.ds(pl.multiple_of(start + dr2 * yy, dr2), dr2)
+
+    us = take(ny)
+    for k in yk:
+        push(wtmp.at[:, of(ypeer(k))], wy.at[k - 1], us + k - 1, at(z, ypeer(k)))
+    dqo[:, lanes(p)] = dqb[rows(T * p)]
+    arrive(rq, qs)
+    dqo[:, lanes(o)] = rq[...]
+    total = wtmp[:, of(y)]
+    for k in yk:
+        arrive(wy.at[k - 1], us + k - 1)
+        total = total + wy[k - 1]
+    wsum[...] = total
     ws = take(1)
-    push(wsend, wrecv, ws, mate)
-    ours = pl.ds(pl.multiple_of(start + dr * p, dr), dr)
-    wko[:, lanes(p)] = wtmp[0, ours]
-    wqo[:, lanes(p)] = wtmp[1, ours]
+    push(wsum.at[:, pl.ds(pl.multiple_of(dr * o, dr), dr)], wrecv, ws, mate)
+    ours = pl.ds(pl.multiple_of(dr * p, dr), dr)
+    wko[:, lanes(p)] = wsum[0, ours]
+    wqo[:, lanes(p)] = wsum[1, ours]
 
     for k in reversed(zk):
         arrive(relz.at[zpeer(nz - k)], ls + k - 1)
-    relo[y] = relz[...].reshape(nz * rb, T).astype(bf16)
+    relo[y] = relz[...].astype(f32).reshape(nz * rb, T).astype(bf16)
     ms = take(ny)
     es = take(ny)
     for k in yk:
         push(relo.at[y], relo.at[y], ms + k - 1, at(z, ypeer(k)))
     push(relo.at[y], relq.at[y], es, mate)
 
-    dqo[:, lanes(p)] = dqb[rows(T * p)]
-    arrive(rq, qs)
-    dqo[:, lanes(o)] = rq[...]
     row = rows(2 * HALO * T + T * p)
     rkv[HALO, p, 0] = dkb[row]
     rkv[HALO, p, 1] = dvb[row]
@@ -499,7 +516,8 @@
     buckets, width = rel_emb.shape
     span = bucket_table.shape[0]
     rb = buckets // nc
-    dr = width // nc // 2
+    dr2 = width // nc
+    dr = dr2 // 2
     keys_in = TILES * T
     shape = jax.ShapeDtypeStruct
     tab = bucket_table.reshape(1, -1)
@@ -545,19 +563,20 @@
             pltpu.VMEM((2 * T, T), bf16),
             pltpu.VMEM((T, span), f32),
             pltpu.VMEM((T, span + 4 * T), f32),
-            pltpu.VMEM((nc, 2 * rb, T), bf16),
+            pltpu.VMEM((2, buckets, T), bf16),
             pltpu.VMEM((5, 2, 2, T, T), bf16),
             pltpu.VMEM((T, T), bf16),
-            pltpu.VMEM((ny, nz, 2 * rb, T), bf16),
+            pltpu.VMEM((2, ny, nz * rb, T), bf16),
             pltpu.VMEM((nz, 2 * rb, T), bf16),
             pltpu.VMEM((nz, 2 * rb, T), bf16),
             pltpu.VMEM((2 * rb, T), bf16),
-            pltpu.VMEM((nc, 2 * rb, T), bf16),
+            pltpu.VMEM((nz, 2 * rb, T), bf16),
             pltpu.VMEM((2 * nx, rb, T), f32),
             pltpu.VMEM((2 * nx, rb, T), f32),
-            pltpu.VMEM((nz, rb, T), f32),
+            pltpu.VMEM((nz, rb, T), bf16),
             pltpu.VMEM((2, T, T), f32),
-            pltpu.VMEM((2, dr, T), f32),
+            pltpu.VMEM((ny, 2, dr2, T), f32),
+            pltpu.VMEM((2, dr2, T), f32),
             pltpu.VMEM((2, dr, T), f32),
             pltpu.SemaphoreType.DMA((144,)),
             pltpu.SemaphoreType.DMA((144,)),

time: 66.5 us -> 65.8 us (0.989)
  no operation moved by 1% of the time
where the time goes in v5:
time: 65.8 us; the launch traced here: 65.6 us
  Pallas kernels  65 us (99%)
    pallas_call x1, Pallas kernels, body(): pl.pallas_call(functools.partial(whole_kernel, nz, ny, nx), out_shape=(sh...  63 us
    pallas_call x1, Pallas kernels, body(): pl.pallas_call(copy_kernel, out_shape=(shape((T, 2 * T), bf16), shape((T,...  1.97 us

profile of v5, /device:TPU:1, one launch (start us, length us, event | category | flops | bytes accessed | tf_op | source)
XLA Modules:
  0.0 65.6 jit_solution(120325203495144203)
XLA Ops:
  0.6 63.0 %whole.1 = (bf16[128,256]{1,0:T(8,128)(2,1)}, bf16[128,256]{1,0:T(8,128)(2,1)}, bf16[128,256]{1,0:T(8,128)(2,1)}, bf16[4,128,128]{2,1,0:T(8,128)(2,1)}, bf16[4,1...) custom-call(bf16[128,256]{1,0:T(8,128)(2,1)} %q_ref.1, bf16[128,256]{1,0:T(8,128)(2,1)} %k_ref.1, ...), custom_call_target="tpu_custom_call" | custom-call | tf_op jit(solution)/shard_map/whole/pallas_call | solution.py:525
  63.7 2.0 %results.1 = (bf16[128,256]{1,0:T(8,128)(2,1)}, bf16[128,256]{1,0:T(8,128)(2,1)}, bf16[128,256]{1,0:T(8,128)(2,1)}, f32[512,256]{1,0:T(8,128)}, f32[8,256]{1,0:T(8,128)}, /*index=5*/f32[8,256]{1,0:T(8,128)}) custom-call(bf16[128,256]{1,0:T(8,128)(2,1)} %get-tuple-element.13.dq, bf16[128,256]{1,0:T(8,128)(2,1)} %get-tuple-element.14.dk, ...), custom_call_target="tpu_custom_call" | custom-call | tf_op jit(solution)/shard_map/results/pallas_call | solution.py:590

commit v6 on v5

--- a/solution.py
+++ b/solution.py
@@ -57,6 +57,10 @@
     return pltpu.roll(x, first, 1, stride=1, stride_axis=0)
 
 
+def by_distance(nz):
+    return sorted(range(nz), key=lambda k: min(k, nz - k))
+
+
 def head_only(x, h):
     lane = lax.broadcasted_iota(jnp.int32, x.shape, 1)
     return jnp.where((lane < HD) if h == 0 else (lane >= HD), x, jnp.zeros_like(x))
@@ -72,7 +76,7 @@
     dqo, dko, dvo, relo, relq, wko, wqo,
     rel_v, wv, qw, gw, kw, vw, pb, oht, q2, g2, k2, pqr, qrt, krt,
     sc, dp, prb, dsb, dsr, skb, dsa, ska, dkb, dvb, dqb, gt, ht,
-    bp, rkv, rq, yrecv, zsend, zrecv, own, ag, xpart, xrecv, relz,
+    bp, rkv, rq, yrecv, zsend, zrecv, own, ag, xpart, xrecv,
     wtmp, wy, wsum, wrecv, send, recv, local, known,
 ):
     nc = nz * ny
@@ -111,6 +115,7 @@
     yk = sorted(range(1, ny), key=lambda k: -min(k, ny - k))
     zk = sorted(range(1, nz), key=lambda k: -min(k, nz - k))
     mk = range(1, 2 * nx)
+    order = by_distance(nz)
 
     for k in (1, nz - 1):
         greet(at(zpeer(k), y))
@@ -383,10 +388,6 @@
     for k in zk:
         push(zsend.at[zpeer(k)], zrecv.at[k - 1], zs + k - 1, at(zpeer(k), y))
 
-    for j in far_first:
-        dk = dot(dsr[0, tile(j)], q2[0]) + dot(dsr[1, tile(j)], q2[1])
-        dk = dk + dot(skb[0, tile(j)], pqr[0, band(j)]) + dot(skb[1, tile(j)], pqr[1, band(j)])
-        dkb[tile(j)] = dot(flip, (SCALE * dk).astype(bf16)).astype(bf16)
     rs = take(20)
 
     def give_back(grad, i):
@@ -400,6 +401,10 @@
     qs = take(1)
     push(dqb.at[rows(T * o)], rq, qs, mate)
     give_back(dvb, 1)
+    for j in far_first:
+        dk = dot(dsr[0, tile(j)], q2[0]) + dot(dsr[1, tile(j)], q2[1])
+        dk = dk + dot(skb[0, tile(j)], pqr[0, band(j)]) + dot(skb[1, tile(j)], pqr[1, band(j)])
+        dkb[tile(j)] = dot(flip, (SCALE * dk).astype(bf16)).astype(bf16)
     give_back(dkb, 0)
 
     part = zsend[z].astype(f32)
@@ -426,10 +431,10 @@
     for k in mk:
         arrive(xrecv.at[k - 1], xs + k - 1)
         total = total + xrecv[k - 1]
-    relz[z] = total.astype(bf16)
+    relo[y, 0] = total.astype(bf16)
     ls = take(nz)
     for k in zk:
-        push(relz.at[z], relz.at[z], ls + k - 1, at(zpeer(k), y))
+        push(relo.at[y, 0], relo.at[y, order.index(k)], ls + k - 1, at(zpeer(k), y))
 
     for k in reversed(zk):
         arrive(ag.at[zpeer(nz - k)], gs + k - 1)
@@ -446,6 +451,23 @@
     us = take(ny)
     for k in yk:
         push(wtmp.at[:, of(ypeer(k))], wy.at[k - 1], us + k - 1, at(z, ypeer(k)))
+
+    ms = take(2 * ny)
+    es = take(2 * ny)
+
+    def piece(part):
+        return pl.ds(part * (nz // 2), nz // 2)
+
+    def spread(part):
+        for i in range(part * (nz // 2), (part + 1) * (nz // 2)):
+            if i:
+                arrive(relo.at[y, i], ls + order[i] - 1)
+        for k in yk:
+            push(relo.at[y, piece(part)], relo.at[y, piece(part)],
+                 ms + part * ny + k - 1, at(z, ypeer(k)))
+        push(relo.at[y, piece(part)], relq.at[y, piece(part)], es + part * ny, mate)
+
+    spread(0)
     dqo[:, lanes(p)] = dqb[rows(T * p)]
     arrive(rq, qs)
     dqo[:, lanes(o)] = rq[...]
@@ -460,14 +482,13 @@
     wko[:, lanes(p)] = wsum[0, ours]
     wqo[:, lanes(p)] = wsum[1, ours]
 
-    for k in reversed(zk):
-        arrive(relz.at[zpeer(nz - k)], ls + k - 1)
-    relo[y] = relz[...].astype(f32).reshape(nz * rb, T).astype(bf16)
-    ms = take(ny)
-    es = take(ny)
-    for k in yk:
-        push(relo.at[y], relo.at[y], ms + k - 1, at(z, ypeer(k)))
-    push(relo.at[y], relq.at[y], es, mate)
+    spread(1)
+
+    for part in range(2):
+        for k in reversed(yk):
+            yy = ypeer(ny - k)
+            arrive(relo.at[yy, piece(part)], ms + part * ny + k - 1)
+            push(relo.at[yy, piece(part)], relq.at[yy, piece(part)], es + part * ny + k, mate)
 
     row = rows(2 * HALO * T + T * p)
     rkv[HALO, p, 0] = dkb[row]
@@ -485,26 +506,30 @@
                 x = x + rkv[d, pp, i].astype(f32)
             out[:, tile(pp)] = x.astype(bf16)
 
-    for k in reversed(yk):
-        arrive(relo.at[ypeer(ny - k)], ms + k - 1)
-        push(relo.at[ypeer(ny - k)], relq.at[ypeer(ny - k)], es + k, mate)
     arrive(wrecv, ws)
     wko[:, lanes(o)] = wrecv[0]
     wqo[:, lanes(o)] = wrecv[1]
-    arrive(relq.at[y], es)
-    for k in reversed(yk):
-        arrive(relq.at[ypeer(ny - k)], es + k)
+    for part in range(2):
+        arrive(relq.at[y, piece(part)], es + part * ny)
+        for k in reversed(yk):
+            arrive(relq.at[ypeer(ny - k), piece(part)], es + part * ny + k)
     for copy in sent:
         copy.wait_send()
 
 
-def copy_kernel(dq, dk, dv, rel, relq, wk, wq, dqo, dko, dvo, relo, wqo, wko):
-    p = lax.rem(lax.axis_index("seq"), 2)
+def copy_kernel(ny, dq, dk, dv, rel, relq, wk, wq, dqo, dko, dvo, relo, wqo, wko):
+    nz, rb = rel.shape[1:3]
+    seq = lax.axis_index("seq")
+    p, z = lax.rem(seq, 2), seq // (2 * ny)
     dqo[...] = dq[...]
     dko[...] = dk[...]
     dvo[...] = dv[...]
-    relo[:, lanes(p)] = rel[...].reshape(relo.shape[0], T).astype(f32)
-    relo[:, lanes(1 - p)] = relq[...].reshape(relo.shape[0], T).astype(f32)
+    for i, k in enumerate(by_distance(nz)):
+        zz = lax.rem(z - k + nz, nz)
+        for yy in range(ny):
+            row = pl.ds(pl.multiple_of((yy * nz + zz) * rb, rb), rb)
+            relo[row, lanes(p)] = rel[yy, i].astype(f32)
+            relo[row, lanes(1 - p)] = relq[yy, i].astype(f32)
     wqo[...] = wq[...]
     wko[...] = wk[...]
 
@@ -528,8 +553,8 @@
             shape((T, 2 * T), bf16),
             shape((T, 2 * T), bf16),
             shape((T, 2 * T), bf16),
-            shape((ny, nz * rb, T), bf16),
-            shape((ny, nz * rb, T), bf16),
+            shape((ny, nz, rb, T), bf16),
+            shape((ny, nz, rb, T), bf16),
             shape((dr, 2 * T), f32),
             shape((dr, 2 * T), f32),
         ),
@@ -573,7 +598,6 @@
             pltpu.VMEM((nz, 2 * rb, T), bf16),
             pltpu.VMEM((2 * nx, rb, T), f32),
             pltpu.VMEM((2 * nx, rb, T), f32),
-            pltpu.VMEM((nz, rb, T), bf16),
             pltpu.VMEM((2, T, T), f32),
             pltpu.VMEM((ny, 2, dr2, T), f32),
             pltpu.VMEM((2, dr2, T), f32),
@@ -588,7 +612,7 @@
     )(queries, keys, values, out_grad, rel_emb, w_query, w_key, tab, lens)
     return tuple(
         pl.pallas_call(
-            copy_kernel,
+            functools.partial(copy_kernel, ny),
             out_shape=(
                 shape((T, 2 * T), bf16),
                 shape((T, 2 * T), bf16),

time: 65.8 us -> 65 us (0.988)
  Pallas kernels: 65 us -> 64.2 us
    pallas_call x1, Pallas kernels: 63 us -> 62.1 us  [body(): pl.pallas_call(functools.partial(whole_kernel, nz, ny, nx), out_shape=(sh...]
where the time goes in v6:
time: 65 us; the launch traced here: 64.8 us
  Pallas kernels  64.2 us (99%)
    pallas_call x1, Pallas kernels, body(): pl.pallas_call(functools.partial(whole_kernel, nz, ny, nx), out_shape=(sh...  62.1 us
    pallas_call x1, Pallas kernels, body(): pl.pallas_call(functools.partial(copy_kernel, ny), out_shape=(shape((T, 2...  2.13 us

profile of v6, /device:TPU:1, one launch (start us, length us, event | category | flops | bytes accessed | tf_op | source)
XLA Modules:
  0.0 64.8 jit_solution(1142318366728897492)
XLA Ops:
  0.6 62.1 %whole.1 = (bf16[128,256]{1,0:T(8,128)(2,1)}, bf16[128,256]{1,0:T(8,128)(2,1)}, bf16[128,256]{1,0:T(8,128)(2,1)}, bf16[4,16,8,128]{3,2,1,0:T(8,128)(2,1)}, bf16[...) custom-call(bf16[128,256]{1,0:T(8,128)(2,1)} %q_ref.1, bf16[128,256]{1,0:T(8,128)(2,1)} %k_ref.1, ...), custom_call_target="tpu_custom_call" | custom-call | tf_op jit(solution)/shard_map/whole/pallas_call | solution.py:550
  62.7 2.1 %results.1 = (bf16[128,256]{1,0:T(8,128)(2,1)}, bf16[128,256]{1,0:T(8,128)(2,1)}, bf16[128,256]{1,0:T(8,128)(2,1)}, f32[512,256]{1,0:T(8,128)}, f32[8,256]{1,0:T(8,128)}, /*index=5*/f32[8,256]{1,0:T(8,128)}) custom-call(bf16[128,256]{1,0:T(8,128)(2,1)} %get-tuple-element.13.dq, bf16[128,256]{1,0:T(8,128)(2,1)} %get-tuple-element.14.dk, ...), custom_call_target="tpu_custom_call" | custom-call | tf_op jit(solution)/shard_map/results/pallas_call | solution.py:614

commit v7 on v6

--- a/solution.py
+++ b/solution.py
@@ -117,13 +117,13 @@
     mk = range(1, 2 * nx)
     order = by_distance(nz)
 
+    for d in (-1, 1):
+        for pp in range(2):
+            greet(2 * chip(d) + pp)
     for k in (1, nz - 1):
         greet(at(zpeer(k), y))
     for k in yk:
         greet(at(z, ypeer(k)))
-    for d in (-1, 1):
-        for pp in range(2):
-            greet(2 * chip(d) + pp)
     for k in mk:
         greet(2 * c + lax.rem(mpeer(k), 2), mpeer(k) // 2)
     greet(mate)
@@ -309,21 +309,29 @@
     passed(0, kw)
     for j in outer:
         score(j)
-    passed(1, vw)
-    for j in outer:
-        through_values(j)
-
-    inv, row_dot = [], []
+
+    totals, alongs = [], []
     for h in range(2):
         high_score = jnp.max(top[h], axis=0, keepdims=True)
         total = jnp.zeros((8, 2 * T), f32)
         along = jnp.zeros((8, 2 * T), f32)
-        for j in range(TILES):
+        for j in inner + outer:
             x = jnp.exp(sc[h, tile(j)] - high_score)
             sc[h, tile(j)] = x
             total = total + fold(x, jnp.sum)
-            along = along + fold(x * dp[h, tile(j)], jnp.sum)
-        inv.append(1.0 / jnp.sum(total, axis=0, keepdims=True))
+            if j in inner:
+                along = along + fold(x * dp[h, tile(j)], jnp.sum)
+        totals.append(total)
+        alongs.append(along)
+    passed(1, vw)
+    inv, row_dot = [], []
+    for h in range(2):
+        along = alongs[h]
+        for j in outer:
+            x = dot(vw[tile(j)], g2[h], 1, 1)
+            dp[h, tile(j)] = x
+            along = along + fold(sc[h, tile(j)] * x, jnp.sum)
+        inv.append(1.0 / jnp.sum(totals[h], axis=0, keepdims=True))
         row_dot.append(jnp.sum(along, axis=0, keepdims=True) * inv[h])
 
     for h in range(2):
@@ -483,12 +491,6 @@
     wqo[:, lanes(p)] = wsum[1, ours]
 
     spread(1)
-
-    for part in range(2):
-        for k in reversed(yk):
-            yy = ypeer(ny - k)
-            arrive(relo.at[yy, piece(part)], ms + part * ny + k - 1)
-            push(relo.at[yy, piece(part)], relq.at[yy, piece(part)], es + part * ny + k, mate)
 
     row = rows(2 * HALO * T + T * p)
     rkv[HALO, p, 0] = dkb[row]
@@ -506,6 +508,16 @@
                 x = x + rkv[d, pp, i].astype(f32)
             out[:, tile(pp)] = x.astype(bf16)
 
+    older = len(sent) - ny
+    for copy in sent[:older]:
+        copy.wait_send()
+
+    for part in range(2):
+        for k in reversed(yk):
+            yy = ypeer(ny - k)
+            arrive(relo.at[yy, piece(part)], ms + part * ny + k - 1)
+            push(relo.at[yy, piece(part)], relq.at[yy, piece(part)], es + part * ny + k, mate)
+
     arrive(wrecv, ws)
     wko[:, lanes(o)] = wrecv[0]
     wqo[:, lanes(o)] = wrecv[1]
@@ -513,7 +525,7 @@
         arrive(relq.at[y, piece(part)], es + part * ny)
         for k in reversed(yk):
             arrive(relq.at[ypeer(ny - k), piece(part)], es + part * ny + k)
-    for copy in sent:
+    for copy in sent[older:]:
         copy.wait_send()
 
 

time: 65 us -> 64.8 us (level)
  no operation moved by 1% of the time
where the time goes in v7:
time: 64.8 us; the launch traced here: 64.6 us
  Pallas kernels  64 us (99%)
    pallas_call x1, Pallas kernels, body(): pl.pallas_call(functools.partial(whole_kernel, nz, ny, nx), out_shape=(sh...  61.8 us
    pallas_call x1, Pallas kernels, body(): pl.pallas_call(functools.partial(copy_kernel, ny), out_shape=(shape((T, 2...  2.13 us

profile of v7, /device:TPU:1, one launch (start us, length us, event | category | flops | bytes accessed | tf_op | source)
XLA Modules:
  0.0 64.6 jit_solution(16074714137697345790)
XLA Ops:
  0.6 61.8 %whole.1 = (bf16[128,256]{1,0:T(8,128)(2,1)}, bf16[128,256]{1,0:T(8,128)(2,1)}, bf16[128,256]{1,0:T(8,128)(2,1)}, bf16[4,16,8,128]{3,2,1,0:T(8,128)(2,1)}, bf16[...) custom-call(bf16[128,256]{1,0:T(8,128)(2,1)} %q_ref.1, bf16[128,256]{1,0:T(8,128)(2,1)} %k_ref.1, ...), custom_call_target="tpu_custom_call" | custom-call | tf_op jit(solution)/shard_map/whole/pallas_call | solution.py:562
  62.5 2.1 %results.1 = (bf16[128,256]{1,0:T(8,128)(2,1)}, bf16[128,256]{1,0:T(8,128)(2,1)}, bf16[128,256]{1,0:T(8,128)(2,1)}, f32[512,256]{1,0:T(8,128)}, f32[8,256]{1,0:T(8,128)}, /*index=5*/f32[8,256]{1,0:T(8,128)}) custom-call(bf16[128,256]{1,0:T(8,128)(2,1)} %get-tuple-element.13.dq, bf16[128,256]{1,0:T(8,128)(2,1)} %get-tuple-element.14.dk, ...), custom_call_target="tpu_custom_call" | custom-call | tf_op jit(solution)/shard_map/results/pallas_call | solution.py:626

commit v8 on v7

--- a/solution.py
+++ b/solution.py
@@ -240,7 +240,6 @@
     for copy in loads[:3]:
         copy.wait()
     pos_key = dot(rel_v[...], wv[0]).astype(bf16)
-    pass_on(0, kw)
     pos_query = dot(rel_v[...], wv[1]).astype(bf16)
     pb[...] = dot(onehot, jnp.concatenate([pos_key, pos_query], 1)).astype(bf16)
     for h in range(2):
@@ -248,12 +247,12 @@
         pqr[h, 2 * T : 2 * T + span] = head_only(pb[:, T:], h)
         pqr[h, 2 * T + span :] = jnp.zeros((2 * T, T), bf16)
     ht[...] = jnp.zeros_like(ht)
+    pass_on(0, kw)
 
     hear(0)
     tell(1)
     for copy in loads[3:]:
         copy.wait()
-    pass_on(1, vw)
     arrive(qw.at[rows(T * o)], near)
     arrive(gw.at[rows(T * o)], near + 1)
 
@@ -271,6 +270,7 @@
             for j in range(9):
                 sc[h, tile(r + j), tile(r)] = jnp.transpose(a[:, tile(j)])
 
+    pass_on(1, vw)
     arrive(kw.at[rows(2 * HALO * T + T * o)], near + 2)
     arrive(vw.at[rows(2 * HALO * T + T * o)], near + 3)
 

time: 64.8 us -> 65 us (level)
  no operation moved by 1% of the time
where the time goes in v8:
time: 65 us; the launch traced here: 64.8 us
  Pallas kernels  64.2 us (99%)
    pallas_call x1, Pallas kernels, body(): pl.pallas_call(functools.partial(whole_kernel, nz, ny, nx), out_shape=(sh...  62 us
    pallas_call x1, Pallas kernels, body(): pl.pallas_call(functools.partial(copy_kernel, ny), out_shape=(shape((T, 2...  2.13 us

profile of v8, /device:TPU:1, one launch (start us, length us, event | category | flops | bytes accessed | tf_op | source)
XLA Modules:
  0.0 64.8 jit_solution(16409549632650419998)
XLA Ops:
  0.6 62.0 %whole.1 = (bf16[128,256]{1,0:T(8,128)(2,1)}, bf16[128,256]{1,0:T(8,128)(2,1)}, bf16[128,256]{1,0:T(8,128)(2,1)}, bf16[4,16,8,128]{3,2,1,0:T(8,128)(2,1)}, bf16[...) custom-call(bf16[128,256]{1,0:T(8,128)(2,1)} %q_ref.1, bf16[128,256]{1,0:T(8,128)(2,1)} %k_ref.1, ...), custom_call_target="tpu_custom_call" | custom-call | tf_op jit(solution)/shard_map/whole/pallas_call | solution.py:562
  62.7 2.1 %results.1 = (bf16[128,256]{1,0:T(8,128)(2,1)}, bf16[128,256]{1,0:T(8,128)(2,1)}, bf16[128,256]{1,0:T(8,128)(2,1)}, f32[512,256]{1,0:T(8,128)}, f32[8,256]{1,0:T(8,128)}, /*index=5*/f32[8,256]{1,0:T(8,128)}) custom-call(bf16[128,256]{1,0:T(8,128)(2,1)} %get-tuple-element.13.dq, bf16[128,256]{1,0:T(8,128)(2,1)} %get-tuple-element.14.dk, ...), custom_call_target="tpu_custom_call" | custom-call | tf_op jit(solution)/shard_map/results/pallas_call | solution.py:626
